TPU v7x, 512 devices: a whole 4x4x16 slice. The times are simulated.
512 devices in a mesh: dp: 32 (over y_lo, z), gx: 2 (over core), gy: 8 (over x, y_hi).
Axes of the slice: x: 4, y: 4 (y_hi: 2, y_lo: 2; y = y_hi * 2 + y_lo), z: 16, core: 2. Of those that a mesh axis runs over, the one named last changes fastest.
Arguments:
- field: float32 [32, 64, 1024], P('dp', 'gx', 'gy'), may hold values from -6 to 6
- cotangent: float32 [32, 64, 1024], P('dp', 'gx', 'gy')
- checker: int32 [64, 1024], P('gx', 'gy'), may hold values from 0 to 1, as said below
- weight_in: float32 [3, 3, 32], replicated, may hold values from -2 to 2
- weight_mid: bfloat16 [3, 3, 32, 32], replicated, may hold values from -0.375 to 0.375
- weight_head: bfloat16 [2, 32], replicated, may hold values from -1 to 1
- prior_grads: float32 [32, 2, 8, 23, 9568], P('dp', 'gx', 'gy')
Outputs:
- coupled: float32 [32, 64, 1024], P('dp', 'gx', 'gy')
- field_grad: float32 [32, 64, 1024], P('dp', 'gx', 'gy')
- summed_grads: float32 [24, 9568], replicated
Inputs may be any that keep to these rules, and one draw needn't show every extreme that they name: Each row alternates along the columns: checker[i, j] = (j + p[i]) mod 2, with a parity p[i] of its own for every row i.
All inputs are finite; a program needn't handle non-finite values.
Results may differ from a plain program's by a relative error of at most 0.0034.
Values may be sent and summed in bfloat16 or wider, within the bound.
A program may use at most 64 MiB of HBM per device.

v0:
```python
import math

import jax
import jax.numpy as jnp
from jax import lax
from jax.sharding import PartitionSpec as P


def extended(value, sides, width):
    for axis, dim in sides:
        size, length = (lax.axis_size(axis), value.shape[dim])
        up = [(i, (i + 1) % size) for i in range(size)]
        down = [(j, i) for i, j in up]
        last = lax.slice_in_dim(value, length - width, length, axis=dim)
        initial = lax.slice_in_dim(value, 0, width, axis=dim)
        before = lax.ppermute(last, axis, up)
        after = lax.ppermute(initial, axis, down)
        value = jnp.concatenate([before, value, after], axis=dim)
    return value


def first_conv(padded, weight_in, row_count, col_count):
    total = jnp.zeros((weight_in.shape[2], row_count, col_count), jnp.float32)
    for row_tap in range(3):
        for col_tap in range(3):
            window = padded[row_tap : row_tap + row_count, col_tap : col_tap + col_count]
            total = total + weight_in[row_tap, col_tap][:, None, None] * window[None]
    return total


def on_device(field, cotangent, checker, weight_in, weight_mid, weight_head, prior_grads):
    highest = lax.Precision.HIGHEST
    row_count = field.shape[1]
    col_count = field.shape[2]
    hidden_width = weight_mid.shape[2]
    cell_total = (
        lax.axis_size("dp") * row_count * lax.axis_size("gx") * col_count * lax.axis_size("gy")
    )
    grad_scale = 1.0 / math.sqrt(cell_total)
    values = field[0]
    downstream = cotangent[0]
    frozen = checker.astype(jnp.float32)
    unfrozen = 1.0 - frozen
    masked = frozen * values
    partial_prior = prior_grads.reshape(prior_grads.shape[3], prior_grads.shape[4])
    padded_field = extended(masked, (("gx", 0), ("gy", 1)), 1)
    hidden_one = jnp.tanh(first_conv(padded_field, weight_in, row_count, col_count)).astype(
        jnp.bfloat16
    )
    hidden_pad = extended(hidden_one, (("gx", 1), ("gy", 2)), 1)
    hidden_inner = hidden_pad[:, 1:-1, 1:-1]
    pre_two = jnp.zeros((hidden_width, row_count, col_count), jnp.float32)
    for row_tap in range(3):
        for col_tap in range(3):
            window = hidden_pad[:, row_tap : row_tap + row_count, col_tap : col_tap + col_count]
            pre_two = pre_two + jnp.einsum(
                "oc,cxy->oxy",
                weight_mid[row_tap, col_tap],
                window,
                preferred_element_type=jnp.float32,
            )
    hidden_two = jnp.tanh(pre_two).astype(jnp.bfloat16)
    pair = jnp.einsum("ko,oxy->kxy", weight_head, hidden_two, preferred_element_type=jnp.float32)
    expo = jnp.exp(pair[0])
    coupled = masked + unfrozen * (values * expo + pair[1])
    d_pair = jnp.stack([unfrozen * downstream * values * expo, unfrozen * downstream]).astype(
        jnp.bfloat16
    )
    grad_head = jnp.einsum("kxy,oxy->ko", d_pair, hidden_two, preferred_element_type=jnp.float32)
    d_hidden_two = jnp.einsum(
        "ko,kxy->oxy", weight_head, d_pair, preferred_element_type=jnp.float32
    )
    two_f = hidden_two.astype(jnp.float32)
    d_pre_two = (d_hidden_two * (1.0 - two_f * two_f)).astype(jnp.bfloat16)
    d_two_pad = extended(d_pre_two, (("gx", 1), ("gy", 2)), 1)
    mid_list = []
    d_hidden_one = jnp.zeros((hidden_width, row_count, col_count), jnp.float32)
    for row_tap in range(3):
        for col_tap in range(3):
            window = hidden_pad[:, row_tap : row_tap + row_count, col_tap : col_tap + col_count]
            mid_list.append(
                jnp.einsum("oxy,cxy->oc", d_pre_two, window, preferred_element_type=jnp.float32)
            )
            back_window = d_two_pad[
                :, 2 - row_tap : 2 - row_tap + row_count, 2 - col_tap : 2 - col_tap + col_count
            ]
            d_hidden_one = d_hidden_one + jnp.einsum(
                "oc,oxy->cxy",
                weight_mid[row_tap, col_tap],
                back_window,
                preferred_element_type=jnp.float32,
            )
    one_f = hidden_inner.astype(jnp.float32)
    d_pre_one = d_hidden_one * (1.0 - one_f * one_f)
    in_list = []
    for row_tap in range(3):
        for col_tap in range(3):
            window = padded_field[row_tap : row_tap + row_count, col_tap : col_tap + col_count]
            in_list.append(jnp.einsum("oxy,xy->o", d_pre_one, window, precision=highest))
    d_one_pad = extended(d_pre_one, (("gx", 1), ("gy", 2)), 1)
    d_masked = jnp.zeros((row_count, col_count), jnp.float32)
    for row_tap in range(3):
        for col_tap in range(3):
            back_window = d_one_pad[
                :, 2 - row_tap : 2 - row_tap + row_count, 2 - col_tap : 2 - col_tap + col_count
            ]
            d_masked = d_masked + jnp.einsum(
                "o,oxy->xy", weight_in[row_tap, col_tap], back_window, precision=highest
            )
    field_grad = frozen * downstream + unfrozen * downstream * expo + frozen * d_masked
    layer_grads = (
        jnp.concatenate(
            [jnp.stack(in_list).reshape(-1), jnp.stack(mid_list).reshape(-1), grad_head.reshape(-1)]
        )
        * grad_scale
    )
    stacked = jnp.concatenate([layer_grads[None], partial_prior], axis=0)
    summed_grads = lax.psum(stacked, ("dp", "gx", "gy"))
    return (coupled[None], field_grad[None], summed_grads)


def solution(mesh):
    placed = (
        P("dp", "gx", "gy"),
        P("dp", "gx", "gy"),
        P("gx", "gy"),
        P(),
        P(),
        P(),
        P("dp", "gx", "gy", None, None),
    )
    return jax.shard_map(
        on_device,
        mesh=mesh,
        in_specs=placed,
        out_specs=(P("dp", "gx", "gy"), P("dp", "gx", "gy"), P()),
        check_vma=False,
    )
```

profile of v0, /device:TPU:1, one launch (start us, length us, event | category | flops | bytes accessed | tf_op | source)
XLA Modules:
  0.0 572.6 jit_solution(7181842597088774773)
XLA Ops:
  7.2 0.7 bitcast_multiply_fusion.6
  8.0 8.8 %collective-permute-start = (f32[1,128]{1,0:T(1,128)S(1)}, f32[1,128]{1,0:T(1,128)S(1)}, u32[]{:S(2)}, u32[]{:S(2)}) collective-permute-start(f32[1,128]{1,0:T(1,128)S(1)} %get-tuple-element.38), channel_id=1, source_target_pairs={{0,8},{8,0},{1,9},{9,1},{2,10},{10,2},{3,11},{11,3},{4,12},{12,4},... | collective-permute-start | bytes 1544 | tf_op jit(solution)/shard_map/ppermute | solution.py:16
  16.8 1.9 collective-permute-start.1
  18.7 0.8 slice_bitcast_fusion.8
  19.6 1.3 copy.81
  20.9 1.9 collective-permute-start.2
  22.9 7.0 %collective-permute-start.3 = (f32[34,1]{1,0:T(8,128)S(1)}, f32[34,1]{1,0:T(8,128)S(1)}, u32[]{:S(2)}, u32[]{:S(2)}) collective-permute-start(f32[34,1]{1,0:T(8,128)S(1)} %get-tuple-element.33), channel_id=1, source_target_pairs={{1,0},{2,1},{3,2},{4,3},{5,4},{6,5},{7,6},{0,7},{9,8},{10,9},{11,1... | collective-permute-start | bytes 416 | tf_op jit(solution)/shard_map/ppermute | solution.py:17
  29.9 0.9 collective-permute-done.3
  31.3 3.5 collective-permute-start.4
  34.9 1.9 collective-permute-start.5
  37.0 0.9 collective-permute-done.5
  38.1 1.9 collective-permute-start.6
  40.0 7.5 %collective-permute-start.7 = (bf16[32,34,1]{2,0,1:T(8,128)(2,1)S(1)}, bf16[32,34,1]{2,0,1:T(8,128)(2,1)S(1)}, u32[]{:S(2)}, u32[]{:S(2)}) collective-permute-start(bf16[32,34,1]{2,0,1:T(8,128)(2,1)S(1)} %get-tuple-element.16), channel_id=1, source_target_pairs={{1,0},{2,1},{3,2},{4,3},{5,4},{6,5},{7,6},{0,7},{9,8},{10,9},{11,1... | collective-permute-start | bytes 6536 | tf_op jit(solution)/shard_map/ppermute | solution.py:17
  48.0 4.6 collective-permute-done.6
  52.7 4.9 collective-permute-done.7
  60.0 0.6 fusion.96
  63.3 2.9 collective-permute-start.9
  66.1 1.9 collective-permute-start.8
  68.5 0.7 collective-permute-done.8
  69.4 5.6 collective-permute-start.10
  75.0 1.9 collective-permute-start.11
  77.5 3.5 collective-permute-done.10
  81.0 7.4 %collective-permute-done.11 = bf16[32,34,1]{2,0,1:T(8,128)(2,1)S(1)} collective-permute-done((bf16[32,34,1]{2,0,1:T(8,128)(2,1)S(1)}, bf16[32,34,1]{2,0,1:T(8,128)(2,1)S(1)}, u32[]{:S(2)}, u32[]{:S(2)}) %collective-permute-start.11) | collective-permute-done | bytes 2208 | tf_op jit(solution)/shard_map/ppermute | solution.py:16
  95.8 3.2 collective-permute-start.13
  99.0 1.9 collective-permute-start.12
  100.9 1.0 pad_maximum_fusion.1
  103.1 6.0 %collective-permute-start.14 = (f32[32,34,1]{1,0,2:T(8,128)S(1)}, f32[32,34,1]{1,0,2:T(8,128)S(1)}, u32[]{:S(2)}, u32[]{:S(2)}) collective-permute-start(f32[32,34,1]{1,0,2:T(8,128)S(1)} %copy.33), channel_id=1, source_target_pairs={{1,0},{2,1},{3,2},{4,3},{5,4},{6,5},{7,6},{0,7},{9,8},{10,9},{11,1... | collective-permute-start | bytes 13064 | tf_op jit(solution)/shard_map/ppermute | solution.py:17
  109.5 1.9 collective-permute-start.15
  112.8 4.7 collective-permute-done.15
  121.3 0.6 fusion.86
  121.9 441.7 %all-reduce.2.cloned.1.call-done = f32[24,9568]{1,0:T(8,128)} async-done(((f32[24,9568]{1,0:T(8,128)}), f32[24,9568]{1,0:T(8,128)}) %all-reduce.2.cloned.1.call-update) | async-done | bytes 918544 | tf_op jit(solution)/shard_map/psum | solution.py:118
  563.6 2.2 copy.91
  (101 shorter events, 21.6 us)
Async XLA Ops:
  7.2 52.4 %copy-start = (bf16[2,32]{1,0:T(2,128)(2,1)S(1)}, bf16[2,32]{1,0:T(2,128)(2,1)}, u32[]{:S(2)}) copy-start(bf16[2,32]{1,0:T(2,128)(2,1)} %param.12) | copy-start | bytes 388
  7.2 556.4 %all-reduce.2.cloned.1.call-start = ((), (), s32[]{:S(2)}) async-start(), calls=%async_computation | async-start | bytes 1843200 | tf_op jit(solution)/shard_map/psum | solution.py:118
  8.0 12.9 %collective-permute-start = (f32[1,128]{1,0:T(1,128)S(1)}, f32[1,128]{1,0:T(1,128)S(1)}, u32[]{:S(2)}, u32[]{:S(2)}) collective-permute-start(f32[1,128]{1,0:T(1,128)S(1)} %get-tuple-element.38), channel_id=1, source_target_pairs={{0,8},{8,0},{1,9},{9,1},{2,10},{10,2},{3,11},{11,3},{4,12},{12,4},... | collective-permute-start | bytes 1544 | tf_op jit(solution)/shard_map/ppermute | solution.py:16
  16.8 4.1 collective-permute-start.1
  19.5 17.2 %copy-start.1 = (bf16[3,3,32,32]{3,2,1,0:T(8,128)(2,1)S(1)}, bf16[3,3,32,32]{3,2,1,0:T(8,128)(2,1)}, u32[]{:S(2)}) copy-start(bf16[3,3,32,32]{3,2,1,0:T(8,128)(2,1)} %param.11) | copy-start | bytes 55300
  20.9 8.9 %collective-permute-start.2 = (f32[34,1]{1,0:T(8,128)S(1)}, f32[34,1]{1,0:T(8,128)S(1)}, u32[]{:S(2)}, u32[]{:S(2)}) collective-permute-start(f32[34,1]{1,0:T(8,128)S(1)} %get-tuple-element.32), channel_id=1, source_target_pairs={{0,1},{1,2},{2,3},{3,4},{4,5},{5,6},{6,7},{7,0},{8,9},{9,10},{10,1... | collective-permute-start | bytes 416 | tf_op jit(solution)/shard_map/ppermute | solution.py:16
  22.9 7.9 %collective-permute-start.3 = (f32[34,1]{1,0:T(8,128)S(1)}, f32[34,1]{1,0:T(8,128)S(1)}, u32[]{:S(2)}, u32[]{:S(2)}) collective-permute-start(f32[34,1]{1,0:T(8,128)S(1)} %get-tuple-element.33), channel_id=1, source_target_pairs={{1,0},{2,1},{3,2},{4,3},{5,4},{6,5},{7,6},{0,7},{9,8},{10,9},{11,1... | collective-permute-start | bytes 416 | tf_op jit(solution)/shard_map/ppermute | solution.py:17
  31.3 5.7 collective-permute-start.4
  34.9 3.1 collective-permute-start.5
  38.1 14.5 %collective-permute-start.6 = (bf16[32,34,1]{2,0,1:T(8,128)(2,1)S(1)}, bf16[32,34,1]{2,0,1:T(8,128)(2,1)S(1)}, u32[]{:S(2)}, u32[]{:S(2)}) collective-permute-start(bf16[32,34,1]{2,0,1:T(8,128)(2,1)S(1)} %get-tuple-element.15), channel_id=1, source_target_pairs={{0,1},{1,2},{2,3},{3,4},{4,5},{5,6},{6,7},{7,0},{8,9},{9,10},{10,1... | collective-permute-start | bytes 6536 | tf_op jit(solution)/shard_map/ppermute | solution.py:16
  40.0 17.5 %collective-permute-start.7 = (bf16[32,34,1]{2,0,1:T(8,128)(2,1)S(1)}, bf16[32,34,1]{2,0,1:T(8,128)(2,1)S(1)}, u32[]{:S(2)}, u32[]{:S(2)}) collective-permute-start(bf16[32,34,1]{2,0,1:T(8,128)(2,1)S(1)} %get-tuple-element.16), channel_id=1, source_target_pairs={{1,0},{2,1},{3,2},{4,3},{5,4},{6,5},{7,6},{0,7},{9,8},{10,9},{11,1... | collective-permute-start | bytes 6536 | tf_op jit(solution)/shard_map/ppermute | solution.py:17
  59.2 0.7 copy-start.2
  59.2 0.7 copy-start.4
  59.2 0.7 copy-start.5
  63.3 5.2 collective-permute-start.9
  66.1 3.1 collective-permute-start.8
  69.4 11.6 %collective-permute-start.10 = (bf16[32,34,1]{2,0,1:T(8,128)(2,1)S(1)}, bf16[32,34,1]{2,0,1:T(8,128)(2,1)S(1)}, u32[]{:S(2)}, u32[]{:S(2)}) collective-permute-start(bf16[32,34,1]{2,0,1:T(8,128)(2,1)S(1)} %get-tuple-element.11), channel_id=1, source_target_pairs={{1,0},{2,1},{3,2},{4,3},{5,4},{6,5},{7,6},{0,7},{9,8},{10,9},{11,1... | collective-permute-start | bytes 6536 | tf_op jit(solution)/shard_map/ppermute | solution.py:17
  75.0 13.3 %collective-permute-start.11 = (bf16[32,34,1]{2,0,1:T(8,128)(2,1)S(1)}, bf16[32,34,1]{2,0,1:T(8,128)(2,1)S(1)}, u32[]{:S(2)}, u32[]{:S(2)}) collective-permute-start(bf16[32,34,1]{2,0,1:T(8,128)(2,1)S(1)} %get-tuple-element.12), channel_id=1, source_target_pairs={{0,1},{1,2},{2,3},{3,4},{4,5},{5,6},{6,7},{7,0},{8,9},{9,10},{10,1... | collective-permute-start | bytes 6536 | tf_op jit(solution)/shard_map/ppermute | solution.py:16
  95.4 6.6 %copy-start.3 = (f32[3,3,32]{2,1,0:T(4,128)S(1)}, f32[3,3,32]{2,1,0:T(4,128)}, u32[]{:S(2)}) copy-start(f32[3,3,32]{2,1,0:T(4,128)} %param.10) | copy-start | bytes 3460
  95.8 6.6 %collective-permute-start.13 = (f32[32,1,128]{2,0,1:T(8,128)S(1)}, f32[32,1,128]{2,0,1:T(8,128)S(1)}, u32[]{:S(2)}, u32[]{:S(2)}) collective-permute-start(f32[32,1,128]{2,0,1:T(8,128)S(1)} %get-tuple-element.8), channel_id=1, source_target_pairs={{8,0},{0,8},{9,1},{1,9},{10,2},{2,10},{11,3},{3,11},{12,4},{4,12},... | collective-permute-start | bytes 49160 | tf_op jit(solution)/shard_map/ppermute | solution.py:17
  99.0 3.4 collective-permute-start.12
  103.1 9.1 %collective-permute-start.14 = (f32[32,34,1]{1,0,2:T(8,128)S(1)}, f32[32,34,1]{1,0,2:T(8,128)S(1)}, u32[]{:S(2)}, u32[]{:S(2)}) collective-permute-start(f32[32,34,1]{1,0,2:T(8,128)S(1)} %copy.33), channel_id=1, source_target_pairs={{1,0},{2,1},{3,2},{4,3},{5,4},{6,5},{7,6},{0,7},{9,8},{10,9},{11,1... | collective-permute-start | bytes 13064 | tf_op jit(solution)/shard_map/ppermute | solution.py:17
  109.5 8.1 %collective-permute-start.15 = (f32[32,34,1]{1,0,2:T(8,128)S(1)}, f32[32,34,1]{1,0,2:T(8,128)S(1)}, u32[]{:S(2)}, u32[]{:S(2)}) collective-permute-start(f32[32,34,1]{1,0,2:T(8,128)S(1)} %copy.35), channel_id=1, source_target_pairs={{0,1},{1,2},{2,3},{3,4},{4,5},{5,6},{6,7},{7,0},{8,9},{9,10},{10,1... | collective-permute-start | bytes 13064 | tf_op jit(solution)/shard_map/ppermute | solution.py:16
Sparse Core Ops, SparseCore 0:
  102.5 461.0 all-reduce.1
where the time goes:
time: 573 us
  waiting for transfers between devices  469 us (82%)
  starting transfers between devices  59.9 us (10%)
  matrix products  16.1 us (3%)
  between operations  14.6 us (3%)
  local copies, waits for them, and re-layouts  7.8 us (1%)
    psum x1, waiting for transfers between devices, on_device(): summed_grads = lax.psum(stacked, ('dp', 'gx', 'gy'))  442 us
    ppermute x8, starting transfers between devices, extended(): after = lax.ppermute(initial, axis, down)  36 us
    ppermute x8, starting transfers between devices, extended(): before = lax.ppermute(last, axis, up)  23.8 us
    ppermute x8, waiting for transfers between devices, extended(): before = lax.ppermute(last, axis, up)  17.5 us
  transfers between devices with their start and end apart: 17, of which 9 were waited for; matrix products, arithmetic and copies ran while one was open for 2% of the time, Pallas kernels for 0%

commit v1 on v0

--- a/solution.py
+++ b/solution.py
@@ -1,9 +1,228 @@
+import functools
 import math
 
 import jax
 import jax.numpy as jnp
 from jax import lax
+from jax.experimental import pallas as pl
+from jax.experimental.pallas import tpu as pltpu
 from jax.sharding import PartitionSpec as P
+
+
+MESH = pl.DeviceIdType.MESH
+ROWS = 64
+
+
+def all_reduce_kernel(sizes, prior_ref, layer_ref, out_ref, packed, half_in, xs, xr, zs, zr, fin, wide, sem_c, sem_x, sem_z, sem_t, sem_a, sem_b):
+    n_y, n_gy, n_z = sizes
+    n_p = n_y * n_gy
+    core = lax.axis_index("gx")
+    dp = lax.axis_index("dp")
+    gy = lax.axis_index("gy")
+    z = lax.rem(dp, n_z)
+    p = lax.div(dp, n_z) * n_gy + gy
+    other = 1 - core
+
+    def plane(q):
+        return {"dp": lax.div(q, n_gy) * n_z + z, "gx": core, "gy": lax.rem(q, n_gy)}
+
+    def along(w):
+        return {"dp": dp - z + w, "gx": core, "gy": gy}
+
+    partner = {"dp": dp, "gx": other, "gy": gy}
+    barrier = pltpu.get_barrier_semaphore()
+    pl.semaphore_signal(barrier, inc=1, device_id=partner, device_id_type=MESH)
+
+    def hello_plane(i, _):
+        pl.semaphore_signal(barrier, inc=1, device_id=plane(lax.rem(p + i, n_p)), device_id_type=MESH)
+        return 0
+
+    def hello_along(i, _):
+        pl.semaphore_signal(barrier, inc=1, device_id=along(lax.rem(z + i, n_z)), device_id_type=MESH)
+        return 0
+
+    lax.fori_loop(1, n_p, hello_plane, 0)
+    lax.fori_loop(1, n_z, hello_along, 0)
+
+    n_cols = prior_ref.shape[1]
+    full = n_cols // 128
+    rest = n_cols - full * 128
+    units = packed.shape[0]
+
+    def pack(k, _):
+        at = pl.multiple_of(k * 128, 128)
+        block = jnp.concatenate([prior_ref[:, pl.ds(at, 128)], layer_ref[:, pl.ds(at, 128)]], axis=0)
+        packed[pl.ds(3 * k, 3)] = block.reshape(3, 8, 128)
+        return 0
+
+    lax.fori_loop(0, full, pack, 0)
+    used = 3 * (full + (1 if rest else 0))
+    if rest:
+        block = jnp.concatenate([prior_ref[:, full * 128 :], layer_ref[:, full * 128 :]], axis=0)
+        block = jnp.concatenate([block, jnp.zeros((24, 128 - rest), jnp.float32)], axis=1)
+        packed[3 * full : 3 * full + 3] = block.reshape(3, 8, 128)
+    packed[used:] = jnp.zeros((units - used, 8, 128), jnp.float32)
+
+    pl.semaphore_wait(barrier, 1 + (n_p - 1) + (n_z - 1))
+
+    half = units // 2
+    swap = pltpu.make_async_remote_copy(
+        src_ref=packed.at[pl.ds(other * half, half)], dst_ref=half_in,
+        send_sem=sem_c.at[0], recv_sem=sem_c.at[1], device_id=partner, device_id_type=MESH)
+    swap.start()
+    swap.wait()
+
+    def pair_sum(q, _):
+        value = packed[pl.ds(core * half + 8 * q, 8)] + half_in[pl.ds(8 * q, 8)]
+        xs[q] = value.reshape(ROWS, 128).astype(jnp.bfloat16)
+        return 0
+
+    lax.fori_loop(0, n_p, pair_sum, 0)
+
+    def to_plane(q, slot):
+        return pltpu.make_async_remote_copy(
+            src_ref=xs.at[q], dst_ref=xr.at[slot], send_sem=sem_x.at[0, q], recv_sem=sem_x.at[1, slot],
+            device_id=plane(q), device_id_type=MESH)
+
+    def send_plane(i, _):
+        to_plane(lax.rem(p + i, n_p), p).start()
+        return 0
+
+    lax.fori_loop(1, n_p, send_plane, 0)
+
+    def take_plane(i, total):
+        q = lax.rem(p + n_p - i, n_p)
+        to_plane(q, q).wait_recv()
+        return total + xr[q].astype(jnp.float32)
+
+    total = lax.fori_loop(1, n_p, take_plane, xs[p].astype(jnp.float32))
+    zs[...] = total.astype(jnp.bfloat16).reshape(4, 16, 128)
+
+    def to_along(w, slot):
+        return pltpu.make_async_remote_copy(
+            src_ref=zs.at[lax.rem(w, 4)], dst_ref=zr.at[slot], send_sem=sem_z.at[0, w], recv_sem=sem_z.at[1, slot],
+            device_id=along(w), device_id_type=MESH)
+
+    def send_along(i, _):
+        to_along(lax.rem(z + i, n_z), z).start()
+        return 0
+
+    lax.fori_loop(1, n_z, send_along, 0)
+    tile = lax.rem(z, 4)
+
+    def take_along(i, total):
+        w = lax.rem(z + n_z - i, n_z)
+        to_along(w, w).wait_recv()
+        return total + zr[w].astype(jnp.float32)
+
+    total = lax.fori_loop(1, n_z, take_along, zs[tile].astype(jnp.float32))
+    fin[core, p, tile] = total.astype(jnp.bfloat16)
+
+    def to_four(i, slot):
+        w = z - tile + lax.rem(tile + i, 4)
+        return pltpu.make_async_remote_copy(
+            src_ref=fin.at[core, p, tile], dst_ref=fin.at[core, p, slot], send_sem=sem_t.at[0, i], recv_sem=sem_t.at[1, slot],
+            device_id=along(w), device_id_type=MESH)
+
+    for i in range(1, 4):
+        to_four(i, tile).start()
+    for i in range(1, 4):
+        to_four(i, lax.rem(tile + i, 4)).wait_recv()
+
+    def all_plane(q, slot):
+        return pltpu.make_async_remote_copy(
+            src_ref=fin.at[core, p], dst_ref=fin.at[core, slot], send_sem=sem_a.at[0, q], recv_sem=sem_a.at[1, slot],
+            device_id=plane(q), device_id_type=MESH)
+
+    def to_partner(which, slot):
+        return pltpu.make_async_remote_copy(
+            src_ref=fin.at[core, slot], dst_ref=fin.at[which, slot], send_sem=sem_b.at[0, slot], recv_sem=sem_b.at[1, slot],
+            device_id=partner, device_id_type=MESH)
+
+    def send_all(i, _):
+        all_plane(lax.rem(p + i, n_p), p).start()
+        return 0
+
+    lax.fori_loop(1, n_p, send_all, 0)
+    to_partner(core, p).start()
+
+    def take_all(i, _):
+        q = lax.rem(p + n_p - i, n_p)
+        all_plane(q, q).wait_recv()
+        to_partner(core, q).start()
+        return 0
+
+    lax.fori_loop(1, n_p, take_all, 0)
+
+    def widen_own(q, _):
+        wide[pl.ds((core * n_p + q) * 8, 8)] = fin[core, q].reshape(ROWS, 128).astype(jnp.float32).reshape(8, 8, 128)
+        return 0
+
+    lax.fori_loop(0, n_p, widen_own, 0)
+
+    def widen_other(q, _):
+        to_partner(other, q).wait_recv()
+        wide[pl.ds((other * n_p + q) * 8, 8)] = fin[other, q].reshape(ROWS, 128).astype(jnp.float32).reshape(8, 8, 128)
+        return 0
+
+    lax.fori_loop(0, n_p, widen_other, 0)
+
+    def unpack(k, _):
+        at = pl.multiple_of(k * 128, 128)
+        block = wide[pl.ds(3 * k, 3)].reshape(24, 128)
+        out_ref[:, pl.ds(at, 128)] = pltpu.roll(block, 1, 0)
+        return 0
+
+    lax.fori_loop(0, full, unpack, 0)
+    if rest:
+        block = wide[3 * full : 3 * full + 3].reshape(24, 128)
+        out_ref[:, full * 128 :] = pltpu.roll(block, 1, 0)[:, :rest]
+
+    def drain_plane(i, _):
+        q = lax.rem(p + i, n_p)
+        to_plane(q, p).wait_send()
+        all_plane(q, p).wait_send()
+        return 0
+
+    def drain_along(i, _):
+        to_along(lax.rem(z + i, n_z), z).wait_send()
+        return 0
+
+    def drain_partner(q, _):
+        to_partner(core, q).wait_send()
+        return 0
+
+    lax.fori_loop(1, n_p, drain_plane, 0)
+    lax.fori_loop(1, n_z, drain_along, 0)
+    lax.fori_loop(0, n_p, drain_partner, 0)
+    for i in range(1, 4):
+        to_four(i, tile).wait_send()
+
+
+def all_reduce(prior, layer, sizes):
+    n_y, n_gy, n_z = sizes
+    n_p = n_y * n_gy
+    units = 2 * n_p * 8
+    bf, f32 = jnp.bfloat16, jnp.float32
+    sem = pltpu.SemaphoreType.DMA
+    return pl.pallas_call(
+        functools.partial(all_reduce_kernel, sizes),
+        out_shape=jax.ShapeDtypeStruct((prior.shape[0] + 1, prior.shape[1]), f32),
+        in_specs=[pl.BlockSpec(memory_space=pltpu.VMEM)] * 2,
+        out_specs=pl.BlockSpec(memory_space=pltpu.VMEM),
+        scratch_shapes=[
+            pltpu.VMEM((units, 8, 128), f32),
+            pltpu.VMEM((units // 2, 8, 128), f32),
+            pltpu.VMEM((n_p, ROWS, 128), bf),
+            pltpu.VMEM((n_p, ROWS, 128), bf),
+            pltpu.VMEM((4, 16, 128), bf),
+            pltpu.VMEM((n_z, 16, 128), bf),
+            pltpu.VMEM((2, n_p, 4, 16, 128), bf),
+            pltpu.VMEM((units, 8, 128), f32),
+            sem((2,)), sem((2, n_p)), sem((2, n_z)), sem((2, 4)), sem((2, n_p)), sem((2, n_p)),
+        ],
+        compiler_params=pltpu.CompilerParams(collective_id=0, has_side_effects=True),
+    )(prior, layer)
 
 
 def extended(value, sides, width):
@@ -114,8 +333,8 @@
         )
         * grad_scale
     )
-    stacked = jnp.concatenate([layer_grads[None], partial_prior], axis=0)
-    summed_grads = lax.psum(stacked, ("dp", "gx", "gy"))
+    sizes = (2, lax.axis_size("gy"), lax.axis_size("dp") // 2)
+    summed_grads = all_reduce(partial_prior, layer_grads[None], sizes)
     return (coupled[None], field_grad[None], summed_grads)
 
 

time: 573 us -> 155 us (0.27)
  waiting for transfers between devices: 469 us -> 26.8 us
  Pallas kernels: 0 us -> 39.2 us
  between operations: 14.6 us -> 1.18 us
    psum x1 -> x0, waiting for transfers between devices: 442 us -> none  [on_device(): summed_grads = lax.psum(stacked, ('dp', 'gx', 'gy'))]
    pallas_call x0 -> x1, Pallas kernels: none -> 39.2 us  [all_reduce(): pl.pallas_call(functools.partial(all_reduce_kernel, sizes), out_shape=jax...]
  transfers between devices with their start and end apart: 17 -> 16, of which waited for: 9 -> 8; matrix products, arithmetic and copies ran while one was open for 2% -> 4% of each run, Pallas kernels for 0% -> 25%
where the time goes in v1:
time: 155 us; the launch traced here: 154 us
  starting transfers between devices  58.9 us (38%)
  Pallas kernels  39.2 us (25%)
  waiting for transfers between devices  26.8 us (17%)
  matrix products  16.1 us (10%)
  local copies, waits for them, and re-layouts  7.49 us (5%)
  other arithmetic  4.49 us (3%)
    pallas_call x1, Pallas kernels, all_reduce(): pl.pallas_call(functools.partial(all_reduce_kernel, sizes), out_shape=jax...  39.2 us
    ppermute x8, starting transfers between devices, extended(): after = lax.ppermute(initial, axis, down)  34.1 us
    ppermute x8, starting transfers between devices, extended(): before = lax.ppermute(last, axis, up)  24.8 us
    ppermute x8, waiting for transfers between devices, extended(): before = lax.ppermute(last, axis, up)  16.7 us
    ppermute x8, waiting for transfers between devices, extended(): after = lax.ppermute(initial, axis, down)  10.1 us
    dot_general x9, matrix products, on_device(): jnp.einsum('oxy,xy->o', d_pre_one, window, precision=highest)  4.72 us
    dot_general x9, matrix products, on_device(): jnp.einsum('o,oxy->xy', weight_in[row_tap, col_tap], back_window, precisi...  3.85 us
    unnamed x16, local copies, waits for them, and re-layouts  3.32 us
  transfers between devices with their start and end apart: 16, of which 8 were waited for; matrix products, arithmetic and copies ran while one was open for 4% of the time, Pallas kernels for 25%

profile of v1, /device:TPU:1, one launch (start us, length us, event | category | flops | bytes accessed | tf_op | source)
XLA Modules:
  0.0 154.1 jit_solution(13766320792679162562)
XLA Ops:
  0.6 0.7 bitcast_multiply_fusion.6
  1.4 8.8 %collective-permute-start = (f32[1,128]{1,0:T(1,128)S(1)}, f32[1,128]{1,0:T(1,128)S(1)}, u32[]{:S(2)}, u32[]{:S(2)}) collective-permute-start(f32[1,128]{1,0:T(1,128)S(1)} %get-tuple-element.38), channel_id=1, source_target_pairs={{0,8},{8,0},{1,9},{9,1},{2,10},{10,2},{3,11},{11,3},{4,12},{12,4},... | collective-permute-start | bytes 1544 | tf_op jit(solution)/shard_map/ppermute | solution.py:235
  10.2 1.9 %collective-permute-start.1 = (f32[1,128]{1,0:T(1,128)S(1)}, f32[1,128]{1,0:T(1,128)S(1)}, u32[]{:S(2)}, u32[]{:S(2)}) collective-permute-start(f32[1,128]{1,0:T(1,128)S(1)} %get-tuple-element.39), channel_id=1, source_target_pairs={{8,0},{0,8},{9,1},{1,9},{10,2},{2,10},{11,3},{3,11},{12,4},{4,12},... | collective-permute-start | bytes 1544 | tf_op jit(solution)/shard_map/ppermute | solution.py:236
  12.1 0.8 slice_bitcast_fusion.8
  13.0 2.2 %copy.81 = f32[1,1,1,23,9568]{4,3,2,1,0:T(8,128)} copy(f32[1,1,1,23,9568]{4,2,3,1,0:T(1,128)} %param.13) | data formatting | bytes 1760512
  15.3 1.9 %collective-permute-start.2 = (f32[34,1]{1,0:T(8,128)S(1)}, f32[34,1]{1,0:T(8,128)S(1)}, u32[]{:S(2)}, u32[]{:S(2)}) collective-permute-start(f32[34,1]{1,0:T(8,128)S(1)} %get-tuple-element.32), channel_id=1, source_target_pairs={{0,1},{1,2},{2,3},{3,4},{4,5},{5,6},{6,7},{7,0},{8,9},{9,10},{10,1... | collective-permute-start | bytes 416 | tf_op jit(solution)/shard_map/ppermute | solution.py:235
  17.2 7.0 %collective-permute-start.3 = (f32[34,1]{1,0:T(8,128)S(1)}, f32[34,1]{1,0:T(8,128)S(1)}, u32[]{:S(2)}, u32[]{:S(2)}) collective-permute-start(f32[34,1]{1,0:T(8,128)S(1)} %get-tuple-element.33), channel_id=1, source_target_pairs={{1,0},{2,1},{3,2},{4,3},{5,4},{6,5},{7,6},{0,7},{9,8},{10,9},{11,1... | collective-permute-start | bytes 416 | tf_op jit(solution)/shard_map/ppermute | solution.py:236
  24.2 0.9 collective-permute-done.3
  25.6 3.5 %collective-permute-start.4 = (bf16[32,1,128]{2,0,1:T(8,128)(2,1)S(1)}, bf16[32,1,128]{2,0,1:T(8,128)(2,1)S(1)}, u32[]{:S(2)}, u32[]{:S(2)}) collective-permute-start(bf16[32,1,128]{2,0,1:T(8,128)(2,1)S(1)} %get-tuple-element.19), channel_id=1, source_target_pairs={{0,8},{8,0},{1,9},{9,1},{2,10},{10,2},{3,11},{11,3},{4,12},{12,4},... | collective-permute-start | bytes 24584 | tf_op jit(solution)/shard_map/ppermute | solution.py:235
  29.2 1.9 %collective-permute-start.5 = (bf16[32,1,128]{2,0,1:T(8,128)(2,1)S(1)}, bf16[32,1,128]{2,0,1:T(8,128)(2,1)S(1)}, u32[]{:S(2)}, u32[]{:S(2)}) collective-permute-start(bf16[32,1,128]{2,0,1:T(8,128)(2,1)S(1)} %get-tuple-element.20), channel_id=1, source_target_pairs={{8,0},{0,8},{9,1},{1,9},{10,2},{2,10},{11,3},{3,11},{12,4},{4,12},... | collective-permute-start | bytes 24584 | tf_op jit(solution)/shard_map/ppermute | solution.py:236
  31.3 0.9 collective-permute-done.5
  32.4 1.9 %collective-permute-start.6 = (bf16[32,34,1]{2,0,1:T(8,128)(2,1)S(1)}, bf16[32,34,1]{2,0,1:T(8,128)(2,1)S(1)}, u32[]{:S(2)}, u32[]{:S(2)}) collective-permute-start(bf16[32,34,1]{2,0,1:T(8,128)(2,1)S(1)} %get-tuple-element.15), channel_id=1, source_target_pairs={{0,1},{1,2},{2,3},{3,4},{4,5},{5,6},{6,7},{7,0},{8,9},{9,10},{10,1... | collective-permute-start | bytes 6536 | tf_op jit(solution)/shard_map/ppermute | solution.py:235
  34.4 7.5 %collective-permute-start.7 = (bf16[32,34,1]{2,0,1:T(8,128)(2,1)S(1)}, bf16[32,34,1]{2,0,1:T(8,128)(2,1)S(1)}, u32[]{:S(2)}, u32[]{:S(2)}) collective-permute-start(bf16[32,34,1]{2,0,1:T(8,128)(2,1)S(1)} %get-tuple-element.16), channel_id=1, source_target_pairs={{1,0},{2,1},{3,2},{4,3},{5,4},{6,5},{7,6},{0,7},{9,8},{10,9},{11,1... | collective-permute-start | bytes 6536 | tf_op jit(solution)/shard_map/ppermute | solution.py:236
  42.3 4.7 %collective-permute-done.6 = bf16[32,34,1]{2,0,1:T(8,128)(2,1)S(1)} collective-permute-done((bf16[32,34,1]{2,0,1:T(8,128)(2,1)S(1)}, bf16[32,34,1]{2,0,1:T(8,128)(2,1)S(1)}, u32[]{:S(2)}, u32[]{:S(2)}) %collective-permute-start.6) | collective-permute-done | bytes 2208 | tf_op jit(solution)/shard_map/ppermute | solution.py:235
  47.0 4.9 %collective-permute-done.7 = bf16[32,34,1]{2,0,1:T(8,128)(2,1)S(1)} collective-permute-done((bf16[32,34,1]{2,0,1:T(8,128)(2,1)S(1)}, bf16[32,34,1]{2,0,1:T(8,128)(2,1)S(1)}, u32[]{:S(2)}, u32[]{:S(2)}) %collective-permute-start.7) | collective-permute-done | bytes 2208 | tf_op jit(solution)/shard_map/ppermute | solution.py:236
  54.3 0.6 fusion.96
  57.6 2.9 %collective-permute-start.9 = (bf16[32,1,128]{2,0,1:T(8,128)(2,1)S(1)}, bf16[32,1,128]{2,0,1:T(8,128)(2,1)S(1)}, u32[]{:S(2)}, u32[]{:S(2)}) collective-permute-start(bf16[32,1,128]{2,0,1:T(8,128)(2,1)S(1)} %get-tuple-element.18), channel_id=1, source_target_pairs={{8,0},{0,8},{9,1},{1,9},{10,2},{2,10},{11,3},{3,11},{12,4},{4,12},... | collective-permute-start | bytes 24584 | tf_op jit(solution)/shard_map/ppermute | solution.py:236
  60.5 1.9 %collective-permute-start.8 = (bf16[32,1,128]{2,0,1:T(8,128)(2,1)S(1)}, bf16[32,1,128]{2,0,1:T(8,128)(2,1)S(1)}, u32[]{:S(2)}, u32[]{:S(2)}) collective-permute-start(bf16[32,1,128]{2,0,1:T(8,128)(2,1)S(1)} %get-tuple-element.17), channel_id=1, source_target_pairs={{0,8},{8,0},{1,9},{9,1},{2,10},{10,2},{3,11},{11,3},{4,12},{12,4},... | collective-permute-start | bytes 24584 | tf_op jit(solution)/shard_map/ppermute | solution.py:235
  62.8 0.7 collective-permute-done.8
  63.7 5.6 %collective-permute-start.10 = (bf16[32,34,1]{2,0,1:T(8,128)(2,1)S(1)}, bf16[32,34,1]{2,0,1:T(8,128)(2,1)S(1)}, u32[]{:S(2)}, u32[]{:S(2)}) collective-permute-start(bf16[32,34,1]{2,0,1:T(8,128)(2,1)S(1)} %get-tuple-element.11), channel_id=1, source_target_pairs={{1,0},{2,1},{3,2},{4,3},{5,4},{6,5},{7,6},{0,7},{9,8},{10,9},{11,1... | collective-permute-start | bytes 6536 | tf_op jit(solution)/shard_map/ppermute | solution.py:236
  69.4 1.9 %collective-permute-start.11 = (bf16[32,34,1]{2,0,1:T(8,128)(2,1)S(1)}, bf16[32,34,1]{2,0,1:T(8,128)(2,1)S(1)}, u32[]{:S(2)}, u32[]{:S(2)}) collective-permute-start(bf16[32,34,1]{2,0,1:T(8,128)(2,1)S(1)} %get-tuple-element.12), channel_id=1, source_target_pairs={{0,1},{1,2},{2,3},{3,4},{4,5},{5,6},{6,7},{7,0},{8,9},{9,10},{10,1... | collective-permute-start | bytes 6536 | tf_op jit(solution)/shard_map/ppermute | solution.py:235
  71.8 3.5 %collective-permute-done.10 = bf16[32,34,1]{2,0,1:T(8,128)(2,1)S(1)} collective-permute-done((bf16[32,34,1]{2,0,1:T(8,128)(2,1)S(1)}, bf16[32,34,1]{2,0,1:T(8,128)(2,1)S(1)}, u32[]{:S(2)}, u32[]{:S(2)}) %collective-permute-start.10) | collective-permute-done | bytes 2208 | tf_op jit(solution)/shard_map/ppermute | solution.py:236
  75.3 7.4 %collective-permute-done.11 = bf16[32,34,1]{2,0,1:T(8,128)(2,1)S(1)} collective-permute-done((bf16[32,34,1]{2,0,1:T(8,128)(2,1)S(1)}, bf16[32,34,1]{2,0,1:T(8,128)(2,1)S(1)}, u32[]{:S(2)}, u32[]{:S(2)}) %collective-permute-start.11) | collective-permute-done | bytes 2208 | tf_op jit(solution)/shard_map/ppermute | solution.py:235
  90.0 0.7 broadcast_multiply_fusion.layer_ref
  90.7 3.2 %collective-permute-start.13 = (f32[32,1,128]{2,0,1:T(8,128)S(1)}, f32[32,1,128]{2,0,1:T(8,128)S(1)}, u32[]{:S(2)}, u32[]{:S(2)}) collective-permute-start(f32[32,1,128]{2,0,1:T(8,128)S(1)} %get-tuple-element.8), channel_id=1, source_target_pairs={{8,0},{0,8},{9,1},{1,9},{10,2},{2,10},{11,3},{3,11},{12,4},{4,12},... | collective-permute-start | bytes 49160 | tf_op jit(solution)/shard_map/ppermute | solution.py:236
  93.9 2.1 %collective-permute-start.12 = (f32[32,1,128]{2,0,1:T(8,128)S(1)}, f32[32,1,128]{2,0,1:T(8,128)S(1)}, u32[]{:S(2)}, u32[]{:S(2)}) collective-permute-start(f32[32,1,128]{2,0,1:T(8,128)S(1)} %get-tuple-element.7), channel_id=1, source_target_pairs={{0,8},{8,0},{1,9},{9,1},{2,10},{10,2},{3,11},{11,3},{4,12},{12,4},... | collective-permute-start | bytes 49160 | tf_op jit(solution)/shard_map/ppermute | solution.py:235
  96.4 39.2 %shard_map.94 = f32[24,9568]{1,0:T(8,128)} custom-call(f32[23,9568]{1,0:T(8,128)} %bitcast.366, f32[1,9568]{1,0:T(1,128)} %broadcast_multiply_fusion.layer_ref), custom_call_target="tpu_custom_call" | custom-call | tf_op jit(solution)/shard_map/pallas_call | solution.py:208
  136.3 4.0 %collective-permute-start.14 = (f32[32,34,1]{1,0,2:T(8,128)S(1)}, f32[32,34,1]{1,0,2:T(8,128)S(1)}, u32[]{:S(2)}, u32[]{:S(2)}) collective-permute-start(f32[32,34,1]{1,0,2:T(8,128)S(1)} %copy.33), channel_id=1, source_target_pairs={{1,0},{2,1},{3,2},{4,3},{5,4},{6,5},{7,6},{0,7},{9,8},{10,9},{11,1... | collective-permute-start | bytes 13064 | tf_op jit(solution)/shard_map/ppermute | solution.py:236
  140.7 2.7 %collective-permute-start.15 = (f32[32,34,1]{1,0,2:T(8,128)S(1)}, f32[32,34,1]{1,0,2:T(8,128)S(1)}, u32[]{:S(2)}, u32[]{:S(2)}) collective-permute-start(f32[32,34,1]{1,0,2:T(8,128)S(1)} %copy.35), channel_id=1, source_target_pairs={{0,1},{1,2},{2,3},{3,4},{4,5},{5,6},{6,7},{7,0},{8,9},{9,10},{10,1... | collective-permute-start | bytes 13064 | tf_op jit(solution)/shard_map/ppermute | solution.py:235
  144.9 3.9 %collective-permute-done.15 = f32[32,34,1]{1,0,2:T(8,128)S(1)} collective-permute-done((f32[32,34,1]{1,0,2:T(8,128)S(1)}, f32[32,34,1]{1,0,2:T(8,128)S(1)}, u32[]{:S(2)}, u32[]{:S(2)}) %collective-permute-start.15) | collective-permute-done | bytes 4384 | tf_op jit(solution)/shard_map/ppermute | solution.py:235
  152.5 0.6 fusion.86
  153.2 0.9 copy.91
  (100 shorter events, 21.5 us)
Async XLA Ops:
  0.6 53.3 %copy-start = (bf16[2,32]{1,0:T(2,128)(2,1)S(1)}, bf16[2,32]{1,0:T(2,128)(2,1)}, u32[]{:S(2)}) copy-start(bf16[2,32]{1,0:T(2,128)(2,1)} %param.12) | copy-start | bytes 388
  1.4 13.8 %collective-permute-start = (f32[1,128]{1,0:T(1,128)S(1)}, f32[1,128]{1,0:T(1,128)S(1)}, u32[]{:S(2)}, u32[]{:S(2)}) collective-permute-start(f32[1,128]{1,0:T(1,128)S(1)} %get-tuple-element.38), channel_id=1, source_target_pairs={{0,8},{8,0},{1,9},{9,1},{2,10},{10,2},{3,11},{11,3},{4,12},{12,4},... | collective-permute-start | bytes 1544 | tf_op jit(solution)/shard_map/ppermute | solution.py:235
  10.2 5.0 %collective-permute-start.1 = (f32[1,128]{1,0:T(1,128)S(1)}, f32[1,128]{1,0:T(1,128)S(1)}, u32[]{:S(2)}, u32[]{:S(2)}) collective-permute-start(f32[1,128]{1,0:T(1,128)S(1)} %get-tuple-element.39), channel_id=1, source_target_pairs={{8,0},{0,8},{9,1},{1,9},{10,2},{2,10},{11,3},{3,11},{12,4},{4,12},... | collective-permute-start | bytes 1544 | tf_op jit(solution)/shard_map/ppermute | solution.py:236
  13.0 18.2 %copy-start.2 = (bf16[3,3,32,32]{3,2,1,0:T(8,128)(2,1)S(1)}, bf16[3,3,32,32]{3,2,1,0:T(8,128)(2,1)}, u32[]{:S(2)}) copy-start(bf16[3,3,32,32]{3,2,1,0:T(8,128)(2,1)} %param.11) | copy-start | bytes 55300
  15.3 8.9 %collective-permute-start.2 = (f32[34,1]{1,0:T(8,128)S(1)}, f32[34,1]{1,0:T(8,128)S(1)}, u32[]{:S(2)}, u32[]{:S(2)}) collective-permute-start(f32[34,1]{1,0:T(8,128)S(1)} %get-tuple-element.32), channel_id=1, source_target_pairs={{0,1},{1,2},{2,3},{3,4},{4,5},{5,6},{6,7},{7,0},{8,9},{9,10},{10,1... | collective-permute-start | bytes 416 | tf_op jit(solution)/shard_map/ppermute | solution.py:235
  17.2 7.9 %collective-permute-start.3 = (f32[34,1]{1,0:T(8,128)S(1)}, f32[34,1]{1,0:T(8,128)S(1)}, u32[]{:S(2)}, u32[]{:S(2)}) collective-permute-start(f32[34,1]{1,0:T(8,128)S(1)} %get-tuple-element.33), channel_id=1, source_target_pairs={{1,0},{2,1},{3,2},{4,3},{5,4},{6,5},{7,6},{0,7},{9,8},{10,9},{11,1... | collective-permute-start | bytes 416 | tf_op jit(solution)/shard_map/ppermute | solution.py:236
  25.6 5.7 %collective-permute-start.4 = (bf16[32,1,128]{2,0,1:T(8,128)(2,1)S(1)}, bf16[32,1,128]{2,0,1:T(8,128)(2,1)S(1)}, u32[]{:S(2)}, u32[]{:S(2)}) collective-permute-start(bf16[32,1,128]{2,0,1:T(8,128)(2,1)S(1)} %get-tuple-element.19), channel_id=1, source_target_pairs={{0,8},{8,0},{1,9},{9,1},{2,10},{10,2},{3,11},{11,3},{4,12},{12,4},... | collective-permute-start | bytes 24584 | tf_op jit(solution)/shard_map/ppermute | solution.py:235
  29.2 3.1 %collective-permute-start.5 = (bf16[32,1,128]{2,0,1:T(8,128)(2,1)S(1)}, bf16[32,1,128]{2,0,1:T(8,128)(2,1)S(1)}, u32[]{:S(2)}, u32[]{:S(2)}) collective-permute-start(bf16[32,1,128]{2,0,1:T(8,128)(2,1)S(1)} %get-tuple-element.20), channel_id=1, source_target_pairs={{8,0},{0,8},{9,1},{1,9},{10,2},{2,10},{11,3},{3,11},{12,4},{4,12},... | collective-permute-start | bytes 24584 | tf_op jit(solution)/shard_map/ppermute | solution.py:236
  32.4 14.5 %collective-permute-start.6 = (bf16[32,34,1]{2,0,1:T(8,128)(2,1)S(1)}, bf16[32,34,1]{2,0,1:T(8,128)(2,1)S(1)}, u32[]{:S(2)}, u32[]{:S(2)}) collective-permute-start(bf16[32,34,1]{2,0,1:T(8,128)(2,1)S(1)} %get-tuple-element.15), channel_id=1, source_target_pairs={{0,1},{1,2},{2,3},{3,4},{4,5},{5,6},{6,7},{7,0},{8,9},{9,10},{10,1... | collective-permute-start | bytes 6536 | tf_op jit(solution)/shard_map/ppermute | solution.py:235
  34.4 17.5 %collective-permute-start.7 = (bf16[32,34,1]{2,0,1:T(8,128)(2,1)S(1)}, bf16[32,34,1]{2,0,1:T(8,128)(2,1)S(1)}, u32[]{:S(2)}, u32[]{:S(2)}) collective-permute-start(bf16[32,34,1]{2,0,1:T(8,128)(2,1)S(1)} %get-tuple-element.16), channel_id=1, source_target_pairs={{1,0},{2,1},{3,2},{4,3},{5,4},{6,5},{7,6},{0,7},{9,8},{10,9},{11,1... | collective-permute-start | bytes 6536 | tf_op jit(solution)/shard_map/ppermute | solution.py:236
  53.5 0.7 copy-start.3
  53.5 0.7 copy-start.5
  53.5 0.7 copy-start.6
  57.6 5.2 %collective-permute-start.9 = (bf16[32,1,128]{2,0,1:T(8,128)(2,1)S(1)}, bf16[32,1,128]{2,0,1:T(8,128)(2,1)S(1)}, u32[]{:S(2)}, u32[]{:S(2)}) collective-permute-start(bf16[32,1,128]{2,0,1:T(8,128)(2,1)S(1)} %get-tuple-element.18), channel_id=1, source_target_pairs={{8,0},{0,8},{9,1},{1,9},{10,2},{2,10},{11,3},{3,11},{12,4},{4,12},... | collective-permute-start | bytes 24584 | tf_op jit(solution)/shard_map/ppermute | solution.py:236
  60.5 3.1 %collective-permute-start.8 = (bf16[32,1,128]{2,0,1:T(8,128)(2,1)S(1)}, bf16[32,1,128]{2,0,1:T(8,128)(2,1)S(1)}, u32[]{:S(2)}, u32[]{:S(2)}) collective-permute-start(bf16[32,1,128]{2,0,1:T(8,128)(2,1)S(1)} %get-tuple-element.17), channel_id=1, source_target_pairs={{0,8},{8,0},{1,9},{9,1},{2,10},{10,2},{3,11},{11,3},{4,12},{12,4},... | collective-permute-start | bytes 24584 | tf_op jit(solution)/shard_map/ppermute | solution.py:235
  63.7 11.6 %collective-permute-start.10 = (bf16[32,34,1]{2,0,1:T(8,128)(2,1)S(1)}, bf16[32,34,1]{2,0,1:T(8,128)(2,1)S(1)}, u32[]{:S(2)}, u32[]{:S(2)}) collective-permute-start(bf16[32,34,1]{2,0,1:T(8,128)(2,1)S(1)} %get-tuple-element.11), channel_id=1, source_target_pairs={{1,0},{2,1},{3,2},{4,3},{5,4},{6,5},{7,6},{0,7},{9,8},{10,9},{11,1... | collective-permute-start | bytes 6536 | tf_op jit(solution)/shard_map/ppermute | solution.py:236
  69.4 13.3 %collective-permute-start.11 = (bf16[32,34,1]{2,0,1:T(8,128)(2,1)S(1)}, bf16[32,34,1]{2,0,1:T(8,128)(2,1)S(1)}, u32[]{:S(2)}, u32[]{:S(2)}) collective-permute-start(bf16[32,34,1]{2,0,1:T(8,128)(2,1)S(1)} %get-tuple-element.12), channel_id=1, source_target_pairs={{0,1},{1,2},{2,3},{3,4},{4,5},{5,6},{6,7},{7,0},{8,9},{9,10},{10,1... | collective-permute-start | bytes 6536 | tf_op jit(solution)/shard_map/ppermute | solution.py:235
  87.6 8.4 %copy-start.4 = (f32[3,3,32]{2,1,0:T(4,128)S(1)}, f32[3,3,32]{2,1,0:T(4,128)}, u32[]{:S(2)}) copy-start(f32[3,3,32]{2,1,0:T(4,128)} %param.10) | copy-start | bytes 3460
  90.7 44.9 %collective-permute-start.13 = (f32[32,1,128]{2,0,1:T(8,128)S(1)}, f32[32,1,128]{2,0,1:T(8,128)S(1)}, u32[]{:S(2)}, u32[]{:S(2)}) collective-permute-start(f32[32,1,128]{2,0,1:T(8,128)S(1)} %get-tuple-element.8), channel_id=1, source_target_pairs={{8,0},{0,8},{9,1},{1,9},{10,2},{2,10},{11,3},{3,11},{12,4},{4,12},... | collective-permute-start | bytes 49160 | tf_op jit(solution)/shard_map/ppermute | solution.py:236
  93.9 41.7 %collective-permute-start.12 = (f32[32,1,128]{2,0,1:T(8,128)S(1)}, f32[32,1,128]{2,0,1:T(8,128)S(1)}, u32[]{:S(2)}, u32[]{:S(2)}) collective-permute-start(f32[32,1,128]{2,0,1:T(8,128)S(1)} %get-tuple-element.7), channel_id=1, source_target_pairs={{0,8},{8,0},{1,9},{9,1},{2,10},{10,2},{3,11},{11,3},{4,12},{12,4},... | collective-permute-start | bytes 49160 | tf_op jit(solution)/shard_map/ppermute | solution.py:235
  136.3 8.0 %collective-permute-start.14 = (f32[32,34,1]{1,0,2:T(8,128)S(1)}, f32[32,34,1]{1,0,2:T(8,128)S(1)}, u32[]{:S(2)}, u32[]{:S(2)}) collective-permute-start(f32[32,34,1]{1,0,2:T(8,128)S(1)} %copy.33), channel_id=1, source_target_pairs={{1,0},{2,1},{3,2},{4,3},{5,4},{6,5},{7,6},{0,7},{9,8},{10,9},{11,1... | collective-permute-start | bytes 13064 | tf_op jit(solution)/shard_map/ppermute | solution.py:236
  140.7 8.1 %collective-permute-start.15 = (f32[32,34,1]{1,0,2:T(8,128)S(1)}, f32[32,34,1]{1,0,2:T(8,128)S(1)}, u32[]{:S(2)}, u32[]{:S(2)}) collective-permute-start(f32[32,34,1]{1,0,2:T(8,128)S(1)} %copy.35), channel_id=1, source_target_pairs={{0,1},{1,2},{2,3},{3,4},{4,5},{5,6},{6,7},{7,0},{8,9},{9,10},{10,1... | collective-permute-start | bytes 13064 | tf_op jit(solution)/shard_map/ppermute | solution.py:235
  150.8 2.3 %copy-start.1 = (f32[24,9568]{1,0:T(8,128)S(1)}, f32[24,9568]{1,0:T(8,128)}, u32[]{:S(2)}) copy-start(f32[24,9568]{1,0:T(8,128)} %shard_map.94) | copy-start | bytes 2755588

commit v2 on v1

--- a/solution.py
+++ b/solution.py
@@ -7,7 +7,6 @@
 from jax.experimental import pallas as pl
 from jax.experimental.pallas import tpu as pltpu
 from jax.sharding import PartitionSpec as P
-
 
 MESH = pl.DeviceIdType.MESH
 ROWS = 64
@@ -51,14 +50,14 @@
 
     def pack(k, _):
         at = pl.multiple_of(k * 128, 128)
-        block = jnp.concatenate([prior_ref[:, pl.ds(at, 128)], layer_ref[:, pl.ds(at, 128)]], axis=0)
+        block = jnp.concatenate([prior_ref[:, pl.ds(at, 128)], layer_ref[pl.ds(k, 1), :]], axis=0)
         packed[pl.ds(3 * k, 3)] = block.reshape(3, 8, 128)
         return 0
 
     lax.fori_loop(0, full, pack, 0)
     used = 3 * (full + (1 if rest else 0))
     if rest:
-        block = jnp.concatenate([prior_ref[:, full * 128 :], layer_ref[:, full * 128 :]], axis=0)
+        block = jnp.concatenate([prior_ref[:, full * 128 :], layer_ref[full : full + 1, :rest]], axis=0)
         block = jnp.concatenate([block, jnp.zeros((24, 128 - rest), jnp.float32)], axis=1)
         packed[3 * full : 3 * full + 3] = block.reshape(3, 8, 128)
     packed[used:] = jnp.zeros((units - used, 8, 128), jnp.float32)
@@ -225,117 +224,326 @@
     )(prior, layer)
 
 
-def extended(value, sides, width):
-    for axis, dim in sides:
-        size, length = (lax.axis_size(axis), value.shape[dim])
-        up = [(i, (i + 1) % size) for i in range(size)]
-        down = [(j, i) for i, j in up]
-        last = lax.slice_in_dim(value, length - width, length, axis=dim)
-        initial = lax.slice_in_dim(value, 0, width, axis=dim)
-        before = lax.ppermute(last, axis, up)
-        after = lax.ppermute(initial, axis, down)
-        value = jnp.concatenate([before, value, after], axis=dim)
-    return value
-
-
-def first_conv(padded, weight_in, row_count, col_count):
-    total = jnp.zeros((weight_in.shape[2], row_count, col_count), jnp.float32)
-    for row_tap in range(3):
-        for col_tap in range(3):
-            window = padded[row_tap : row_tap + row_count, col_tap : col_tap + col_count]
-            total = total + weight_in[row_tap, col_tap][:, None, None] * window[None]
-    return total
+def flat_roll(value, offset):
+    return pltpu.roll(value, (-offset) % value.shape[-1], value.ndim - 1)
+
+
+def halves(value):
+    high = value.astype(jnp.bfloat16)
+    return high, (value - high.astype(jnp.float32)).astype(jnp.bfloat16)
+
+
+def nt(a, b, **how):
+    return lax.dot_general(a, b, (((1,), (1,)), ((), ())), preferred_element_type=jnp.float32, **how)
+
+
+def dot(a, b):
+    return jnp.dot(a, b, preferred_element_type=jnp.float32)
+
+
+def lanes_of(shape):
+    return lax.broadcasted_iota(jnp.int32, shape, len(shape) - 1)
+
+
+def layer_kernel(scale, field_ref, cot_ref, check_ref, win_ref, wmid_ref, whead_ref,
+                 coupled_ref, fgrad_ref, layer_ref,
+                 near_f, near_c, near_k, ext, pack_out, pack_in, taps, edge_taps, w9, w2, w3,
+                 xm, xs, xd, xds, cp, pair_rows, t_rows, acc_mid, b_rows, sem_r, sem_p):
+    f32, bf = jnp.float32, jnp.bfloat16
+    dp, core, gy = lax.axis_index("dp"), lax.axis_index("gx"), lax.axis_index("gy")
+    n_gy = lax.axis_size("gy")
+    partner = {"dp": dp, "gx": 1 - core, "gy": gy}
+    left = {"dp": dp, "gx": core, "gy": lax.rem(gy + n_gy - 1, n_gy)}
+    right = {"dp": dp, "gx": core, "gy": lax.rem(gy + 1, n_gy)}
+    barrier = pltpu.get_barrier_semaphore()
+    for who in (partner, left, right):
+        pl.semaphore_signal(barrier, inc=1, device_id=who, device_id_type=MESH)
+
+    for a in range(3):
+        w9[3 * a : 3 * a + 3, 0:32] = win_ref[a]
+    w9[9:16, 0:32] = jnp.zeros((7, 32), f32)
+    eye_f = (lax.broadcasted_iota(jnp.int32, (32, 32), 0) == lanes_of((32, 32))).astype(f32)
+    eye = eye_f.astype(bf)
+    w_taps = w9[:, 0:32]
+    taps_t = nt(eye_f, w_taps, precision=lax.Precision.HIGHEST)
+    th, tl = halves(taps_t)
+    w_one = jnp.concatenate([th, th, tl], axis=1)
+    wh, wl = halves(w_taps)
+    w_back = jnp.concatenate([wh, wh, wl], axis=1)
+    head = whead_ref[...]
+    head_t = nt(eye, head)
+    head_0, head_1 = head_t[:, 0:1], head_t[:, 1:2]
+    for a in range(3):
+        for b in range(3):
+            k = 3 * a + b
+            w2[:, 32 * k : 32 * k + 32] = wmid_ref[a, b]
+            kb = 3 * (2 - a) + b
+            w3[:, 32 * kb : 32 * kb + 32] = wmid_ref[a, b].astype(f32).T.astype(bf)
+
+    pl.semaphore_wait(barrier, 3)
+    swaps = [
+        pltpu.make_async_remote_copy(src_ref=src, dst_ref=dst, send_sem=sem_r.at[0, i], recv_sem=sem_r.at[1, i], device_id=partner, device_id_type=MESH)
+        for i, (src, dst) in enumerate(((field_ref, near_f), (cot_ref, near_c), (check_ref, near_k)))
+    ]
+    for swap in swaps:
+        swap.start()
+    zeros = jnp.zeros((8, 128), f32)
+    for i in range(3):
+        ext[i, 40:48] = zeros
+    ext[0, 4:36] = field_ref[0]
+    ext[1, 4:36] = cot_ref[0]
+    ext[2, 4:36] = check_ref[...].astype(f32)
+    for swap in swaps:
+        swap.wait_recv()
+    ext[0, 0:4], ext[0, 36:40] = near_f[0, 28:32], near_f[0, 0:4]
+    ext[1, 0:4], ext[1, 36:40] = near_c[0, 28:32], near_c[0, 0:4]
+    ext[2, 0:4], ext[2, 36:40] = near_k[28:32].astype(f32), near_k[0:4].astype(f32)
+
+    row_16 = lax.broadcasted_iota(jnp.int32, (16, 128), 0)
+    lane_16 = lanes_of((16, 128))
+    own_lanes = lax.div(lane_16, 8) == row_16
+    for i in range(3):
+        for t in range(3):
+            turned = pltpu.roll(ext[i, 16 * t : 16 * t + 16], 4, 1, stride=8, stride_axis=0)
+            pack_out[3 * i + t : 3 * i + t + 1] = jnp.sum(jnp.where(own_lanes, turned, 0.0), axis=0, keepdims=True)
+    pack_out[9:16] = jnp.zeros((7, 128), f32)
+    posts = [
+        pltpu.make_async_remote_copy(src_ref=pack_out, dst_ref=pack_in.at[i], send_sem=sem_p.at[0, i], recv_sem=sem_p.at[1, i], device_id=who, device_id_type=MESH)
+        for i, who in ((1, left), (0, right))
+    ]
+    for post in posts:
+        post.start()
+    for post in posts:
+        post.wait_recv()
+    column = lax.rem(lane_16, 8)
+    own = pack_out[...]
+    slab_l = jnp.where(column >= 4, own, pack_in[0])
+    slab_r = jnp.where(column < 4, own, pack_in[1])
+
+    def flat(slab, i):
+        return jnp.concatenate([slab[3 * i + t : 3 * i + t + 1] for t in range(3)], axis=1)
+
+    def flat_both(i):
+        return jnp.concatenate([flat(slab_l, i), flat(slab_r, i)], axis=1)
+
+    field_s, cot_s, frozen_s = flat_both(0), flat_both(1), flat_both(2)
+    masked_s = field_s * frozen_s
+
+    def both_rolled(value, offset):
+        return jnp.concatenate([flat_roll(value[:, :384], offset), flat_roll(value[:, 384:], offset)], axis=1)
+
+    def unflat(vector, e):
+        parts = []
+        for t in range(3):
+            spread = jnp.broadcast_to(vector[:, 128 * t : 128 * t + 128], (16, 128))
+            parts.append(jnp.sum(jnp.where(lane_16 == 8 * row_16 + e, spread, 0.0), axis=1, keepdims=True))
+        return jnp.concatenate(parts, axis=0)
+
+    masked = ext[0] * ext[2]
+    lane_48 = lanes_of((48, 128))
+    shifts = (
+        jnp.where(lane_48 == 0, unflat(masked_s[:, :384], 3), pltpu.roll(masked, 1, 1)),
+        masked,
+        jnp.where(lane_48 == 127, unflat(masked_s[:, 384:], 4), pltpu.roll(masked, 127, 1)),
+    )
+    taps[...] = jnp.zeros(taps.shape, f32)
+    edge_taps[...] = jnp.zeros(edge_taps.shape, f32)
+    for a in range(3):
+        for b in range(3):
+            k = 3 * a + b
+            taps[pl.ds(16 + k, 38, stride=16), :] = shifts[b][a : a + 38]
+            edge_taps[k : k + 1, :] = both_rolled(masked_s, 8 * (a - 1) + b - 1)
+
+    def first(tap_values):
+        high, low = halves(tap_values)
+        return jnp.tanh(dot(w_one, jnp.concatenate([high, low, high], axis=0))).astype(bf)
+
+    lane_384 = lanes_of((32, 384))
+
+    def spread_edges(value, back, store):
+        for a in range(3):
+            for b in range(3):
+                k = 3 * a + b
+                offset = 8 * (a - 1) + (1 - b if back else b - 1)
+                store[32 * k : 32 * k + 32, :] = both_rolled(value, offset).astype(bf)
+        mixed = jnp.where(lax.rem(lane_384, 8) == 4, flat_roll(value[:, :384], -1), flat_roll(value[:, 384:], 1))
+        for t in range(3):
+            cp[t] = mixed[:, 128 * t : 128 * t + 128]
+
+    lane_32 = lanes_of((32, 128))
+
+    def spread_row(q, value, back, store):
+        edge = pltpu.roll(cp[lax.div(q, 16)], lax.rem(252 - 8 * lax.rem(q, 16), 128), 1)
+        before = jnp.where(lane_32 == 0, edge, pltpu.roll(value, 1, 1)).astype(bf)
+        after = jnp.where(lane_32 == 127, edge, pltpu.roll(value, 127, 1)).astype(bf)
+        store[q, 0:32] = after if back else before
+        store[q, 32:64] = value.astype(bf)
+        store[q, 64:96] = before if back else after
+
+    one_s = first(edge_taps[...])
+    spread_edges(one_s.astype(f32), False, xs)
+
+    def one_rows(rows):
+        values = jnp.concatenate([taps[pl.ds(pl.multiple_of(16 * q, 16), 16), :] for q in rows], axis=1)
+        out = first(values).astype(f32)
+        for i, q in enumerate(rows):
+            spread_row(q, out[:, 128 * i : 128 * i + 128], False, xm)
+
+    def over_rows(step):
+        def body(i, _):
+            step([4 + 4 * i + n for n in range(4)])
+            return 0
+
+        lax.fori_loop(0, 8, body, 0)
+
+    for q in (0, 39):
+        xm[q] = jnp.zeros((96, 128), bf)
+    one_rows([1, 2, 3, 36])
+    one_rows([37, 38])
+    over_rows(one_rows)
+
+    def second(windows, field, cot, frozen):
+        two = jnp.tanh(dot(w2[...], windows)).astype(bf)
+        pair = dot(head, two)
+        expo = jnp.exp(pair[0:1])
+        open_cot = (1.0 - frozen) * cot
+        d_0 = (open_cot * field * expo).astype(bf)
+        d_1 = open_cot.astype(bf)
+        two_f = two.astype(f32)
+        d_two = (head_0 * d_0.astype(f32) + head_1 * d_1.astype(f32)) * (1.0 - two_f * two_f)
+        return two, pair, d_0, d_1, d_two.astype(bf).astype(f32)
+
+    _, _, _, _, d_two_s = second(xs[...], field_s, cot_s, frozen_s)
+    spread_edges(d_two_s, True, xds)
+
+    def windows_of(store, rows):
+        return jnp.concatenate([store[pl.ds(q - 1, 3)].reshape(288, 128) for q in rows], axis=1)
+
+    def rows_of(i, rows):
+        return jnp.concatenate([ext[i, pl.ds(q, 1), :] for q in rows], axis=1)
+
+    acc_mid[...] = jnp.zeros(acc_mid.shape, f32)
+    b_rows[...] = jnp.zeros(b_rows.shape, f32)
+
+    def two_rows(rows, inner=True):
+        two, pair, d_0, d_1, d_two = second(windows_of(xm, rows), rows_of(0, rows), rows_of(1, rows), rows_of(2, rows))
+        for i, q in enumerate(rows):
+            at = slice(128 * i, 128 * i + 128)
+            spread_row(q, d_two[:, at], True, xd)
+            if inner:
+                pair_rows[pl.ds(pl.multiple_of(8 * q, 8), 2), :] = pair[:, at]
+        if inner:
+            b_rows[297:299, 0:32] += nt(jnp.concatenate([d_0, d_1], axis=0), two)
+
+    for q in (0, 1, 38, 39):
+        xd[q] = jnp.zeros((96, 128), bf)
+    two_rows([2, 3, 36, 37], inner=False)
+    over_rows(two_rows)
+
+    def third(windows, one):
+        one_f = one.astype(f32)
+        d_one = dot(w3[...], windows) * (1.0 - one_f * one_f)
+        high, low = halves(d_one)
+        return high, low, dot(w_back, jnp.concatenate([high, low, high], axis=0))
+
+    _, _, t_s = third(xds[...], one_s)
+
+    def three_rows(rows, inner=True):
+        windows = windows_of(xd, rows)
+        one = jnp.concatenate([xm[q, 32:64] for q in rows], axis=1)
+        high, low, t_values = third(windows, one)
+        for i, q in enumerate(rows):
+            t_rows[pl.ds(pl.multiple_of(16 * q, 16), 16), :] = t_values[:, 128 * i : 128 * i + 128]
+        if inner:
+            acc_mid[...] += nt(windows, one)
+            values = jnp.concatenate([taps[pl.ds(pl.multiple_of(16 * q, 16), 16), :] for q in rows], axis=1)
+            m_high, m_low = halves(values)
+            parts = nt(jnp.concatenate([m_high, m_low], axis=0), jnp.concatenate([high, low], axis=0))
+            parts = parts[0:16] + parts[16:32]
+            b_rows[0:9, 0:32] += (parts[:, 0:32] + parts[:, 32:64])[0:9]
+
+    three_rows([3, 36], inner=False)
+    over_rows(three_rows)
+
+    def column_sum(b):
+        total = None
+        for a in range(3):
+            part = t_rows[pl.ds(16 * (5 - a) + 3 * a + b, 32, stride=16), :]
+            total = part if total is None else total + part
+        return total
+
+    def edge_sum(b, side):
+        total = None
+        for a in range(3):
+            k = 3 * a + b
+            part = flat_roll(t_s[k : k + 1, 384 * side : 384 * side + 384], 8 * (1 - a))
+            total = part if total is None else total + part
+        return total
+
+    lane = lanes_of((32, 128))
+    from_right = unflat(edge_sum(0, 1), 4)[4:36]
+    from_left = unflat(edge_sum(2, 0), 3)[4:36]
+    d_masked = (
+        jnp.where(lane == 127, from_right, pltpu.roll(column_sum(0), 127, 1))
+        + column_sum(1)
+        + jnp.where(lane == 0, from_left, pltpu.roll(column_sum(2), 1, 1))
+    )
+    frozen = check_ref[...].astype(f32)
+    unfrozen = 1.0 - frozen
+    expo = jnp.exp(pair_rows[pl.ds(32, 32, stride=8), :])
+    offset = pair_rows[pl.ds(33, 32, stride=8), :]
+    values, cot = field_ref[0], cot_ref[0]
+    coupled_ref[0] = frozen * values + unfrozen * (values * expo + offset)
+    fgrad_ref[0] = frozen * cot + unfrozen * cot * expo + frozen * d_masked
+
+    for j in range(3):
+        b_rows[9 + 96 * (2 - j) : 9 + 96 * (2 - j) + 96, 0:32] = acc_mid[96 * j : 96 * j + 96]
+    rows = layer_ref.shape[0]
+    layer = b_rows[pl.ds(0, rows, stride=4), :]
+    for g in range(1, 4):
+        layer = layer + pltpu.roll(b_rows[pl.ds(g, rows, stride=4), :], 32 * g, 1)
+    layer_ref[...] = layer * scale
+    for copy in (*swaps, *posts):
+        copy.wait_send()
+
+
+def layer_call(scale, field, cot, checker, weight_in, weight_mid, weight_head):
+    f32, bf = jnp.float32, jnp.bfloat16
+    sem = pltpu.SemaphoreType.DMA
+    vmem = pl.BlockSpec(memory_space=pltpu.VMEM)
+    return pl.pallas_call(
+        functools.partial(layer_kernel, scale),
+        out_shape=(
+            jax.ShapeDtypeStruct(field.shape, f32),
+            jax.ShapeDtypeStruct(field.shape, f32),
+            jax.ShapeDtypeStruct((80, 128), f32),
+        ),
+        in_specs=[vmem] * 6,
+        out_specs=(vmem,) * 3,
+        scratch_shapes=[
+            pltpu.VMEM(field.shape, f32), pltpu.VMEM(field.shape, f32), pltpu.VMEM(checker.shape, jnp.int32),
+            pltpu.VMEM((3, 48, 128), f32),
+            pltpu.VMEM((16, 128), f32), pltpu.VMEM((2, 16, 128), f32),
+            pltpu.VMEM((640, 128), f32), pltpu.VMEM((16, 768), f32),
+            pltpu.VMEM((16, 128), f32), pltpu.VMEM((32, 288), bf), pltpu.VMEM((32, 288), bf),
+            pltpu.VMEM((40, 96, 128), bf), pltpu.VMEM((288, 768), bf),
+            pltpu.VMEM((40, 96, 128), bf), pltpu.VMEM((288, 768), bf),
+            pltpu.VMEM((3, 32, 128), f32),
+            pltpu.VMEM((320, 128), f32), pltpu.VMEM((640, 128), f32),
+            pltpu.VMEM((288, 32), f32), pltpu.VMEM((320, 128), f32),
+            sem((2, 3)), sem((2, 2)),
+        ],
+        compiler_params=pltpu.CompilerParams(collective_id=1, has_side_effects=True),
+    )(field, cot, checker, weight_in, weight_mid, weight_head)
 
 
 def on_device(field, cotangent, checker, weight_in, weight_mid, weight_head, prior_grads):
-    highest = lax.Precision.HIGHEST
-    row_count = field.shape[1]
-    col_count = field.shape[2]
-    hidden_width = weight_mid.shape[2]
-    cell_total = (
-        lax.axis_size("dp") * row_count * lax.axis_size("gx") * col_count * lax.axis_size("gy")
-    )
-    grad_scale = 1.0 / math.sqrt(cell_total)
-    values = field[0]
-    downstream = cotangent[0]
-    frozen = checker.astype(jnp.float32)
-    unfrozen = 1.0 - frozen
-    masked = frozen * values
+    cell_total = field.size * lax.axis_size("dp") * lax.axis_size("gx") * lax.axis_size("gy")
+    scale = 1.0 / math.sqrt(cell_total)
+    coupled, field_grad, layer = layer_call(scale, field, cotangent, checker, weight_in, weight_mid, weight_head)
     partial_prior = prior_grads.reshape(prior_grads.shape[3], prior_grads.shape[4])
-    padded_field = extended(masked, (("gx", 0), ("gy", 1)), 1)
-    hidden_one = jnp.tanh(first_conv(padded_field, weight_in, row_count, col_count)).astype(
-        jnp.bfloat16
-    )
-    hidden_pad = extended(hidden_one, (("gx", 1), ("gy", 2)), 1)
-    hidden_inner = hidden_pad[:, 1:-1, 1:-1]
-    pre_two = jnp.zeros((hidden_width, row_count, col_count), jnp.float32)
-    for row_tap in range(3):
-        for col_tap in range(3):
-            window = hidden_pad[:, row_tap : row_tap + row_count, col_tap : col_tap + col_count]
-            pre_two = pre_two + jnp.einsum(
-                "oc,cxy->oxy",
-                weight_mid[row_tap, col_tap],
-                window,
-                preferred_element_type=jnp.float32,
-            )
-    hidden_two = jnp.tanh(pre_two).astype(jnp.bfloat16)
-    pair = jnp.einsum("ko,oxy->kxy", weight_head, hidden_two, preferred_element_type=jnp.float32)
-    expo = jnp.exp(pair[0])
-    coupled = masked + unfrozen * (values * expo + pair[1])
-    d_pair = jnp.stack([unfrozen * downstream * values * expo, unfrozen * downstream]).astype(
-        jnp.bfloat16
-    )
-    grad_head = jnp.einsum("kxy,oxy->ko", d_pair, hidden_two, preferred_element_type=jnp.float32)
-    d_hidden_two = jnp.einsum(
-        "ko,kxy->oxy", weight_head, d_pair, preferred_element_type=jnp.float32
-    )
-    two_f = hidden_two.astype(jnp.float32)
-    d_pre_two = (d_hidden_two * (1.0 - two_f * two_f)).astype(jnp.bfloat16)
-    d_two_pad = extended(d_pre_two, (("gx", 1), ("gy", 2)), 1)
-    mid_list = []
-    d_hidden_one = jnp.zeros((hidden_width, row_count, col_count), jnp.float32)
-    for row_tap in range(3):
-        for col_tap in range(3):
-            window = hidden_pad[:, row_tap : row_tap + row_count, col_tap : col_tap + col_count]
-            mid_list.append(
-                jnp.einsum("oxy,cxy->oc", d_pre_two, window, preferred_element_type=jnp.float32)
-            )
-            back_window = d_two_pad[
-                :, 2 - row_tap : 2 - row_tap + row_count, 2 - col_tap : 2 - col_tap + col_count
-            ]
-            d_hidden_one = d_hidden_one + jnp.einsum(
-                "oc,oxy->cxy",
-                weight_mid[row_tap, col_tap],
-                back_window,
-                preferred_element_type=jnp.float32,
-            )
-    one_f = hidden_inner.astype(jnp.float32)
-    d_pre_one = d_hidden_one * (1.0 - one_f * one_f)
-    in_list = []
-    for row_tap in range(3):
-        for col_tap in range(3):
-            window = padded_field[row_tap : row_tap + row_count, col_tap : col_tap + col_count]
-            in_list.append(jnp.einsum("oxy,xy->o", d_pre_one, window, precision=highest))
-    d_one_pad = extended(d_pre_one, (("gx", 1), ("gy", 2)), 1)
-    d_masked = jnp.zeros((row_count, col_count), jnp.float32)
-    for row_tap in range(3):
-        for col_tap in range(3):
-            back_window = d_one_pad[
-                :, 2 - row_tap : 2 - row_tap + row_count, 2 - col_tap : 2 - col_tap + col_count
-            ]
-            d_masked = d_masked + jnp.einsum(
-                "o,oxy->xy", weight_in[row_tap, col_tap], back_window, precision=highest
-            )
-    field_grad = frozen * downstream + unfrozen * downstream * expo + frozen * d_masked
-    layer_grads = (
-        jnp.concatenate(
-            [jnp.stack(in_list).reshape(-1), jnp.stack(mid_list).reshape(-1), grad_head.reshape(-1)]
-        )
-        * grad_scale
-    )
     sizes = (2, lax.axis_size("gy"), lax.axis_size("dp") // 2)
-    summed_grads = all_reduce(partial_prior, layer_grads[None], sizes)
-    return (coupled[None], field_grad[None], summed_grads)
+    return coupled, field_grad, all_reduce(partial_prior, layer, sizes)
 
 
 def solution(mesh):

time: 155 us -> 73.5 us (0.47)
  starting transfers between devices: 58.9 us -> 0 us
  Pallas kernels: 39.2 us -> 66.8 us
  waiting for transfers between devices: 26.8 us -> 0 us
  matrix products: 16.1 us -> 0 us
  other arithmetic: 4.49 us -> 0 us
  local copies, waits for them, and re-layouts: 7.49 us -> 5.64 us
    ppermute x16 -> x0, starting transfers between devices: 58.9 us -> none  [the longest x8 34.1 us: extended(): after = lax.ppermute(initial, axis, down)]
    pallas_call x0 -> x1, Pallas kernels: none -> 27.4 us  [layer_call(): pl.pallas_call(functools.partial(layer_kernel, scale), out_shape=(jax.Sha...]
    ppermute x16 -> x0, waiting for transfers between devices: 26.8 us -> none  [the longest x8 16.7 us: extended(): before = lax.ppermute(last, axis, up)]
    dot_general x48 -> x0, matrix products: 16.1 us -> none  [the longest x9 4.72 us: on_device(): jnp.einsum('oxy,xy->o', d_pre_one, window, precision=highest)]
    unnamed x16 -> x8, local copies, waits for them, and re-layouts: 3.32 us -> 5.64 us
  transfers between devices with their start and end apart: 16 -> 0, of which waited for: 8 -> 0; matrix products, arithmetic and copies ran while one was open for 4% -> 0% of each run, Pallas kernels for 25% -> 0%
where the time goes in v2:
time: 73.5 us; the launch traced here: 73.2 us
  Pallas kernels  66.8 us (91%)
  local copies, waits for them, and re-layouts  5.64 us (8%)
    pallas_call x1, Pallas kernels, all_reduce(): pl.pallas_call(functools.partial(all_reduce_kernel, sizes), out_shape=jax...  39.4 us
    pallas_call x1, Pallas kernels, layer_call(): pl.pallas_call(functools.partial(layer_kernel, scale), out_shape=(jax.Sha...  27.4 us
    unnamed x8, local copies, waits for them, and re-layouts  5.64 us

profile of v2, /device:TPU:1, one launch (start us, length us, event | category | flops | bytes accessed | tf_op | source)
XLA Modules:
  0.0 73.2 jit_solution(7327507159479696449)
XLA Ops:
  0.6 27.4 %shard_map.94 = (f32[1,32,128]{2,1,0:T(8,128)}, f32[1,32,128]{2,1,0:T(8,128)}, f32[80,128]{1,0:T(8,128)}) custom-call(f32[1,32,128]{2,1,0:T(8,128)} %field_ref.1, f32[1,32,128]{2,1,0:T(8,128)} %cot_ref.1, s32[32,128]{1,0:T(8,128)} %check_ref.1, f32[3,3,32]{2,1,0:T(4,128)} %win_ref.1, bf16[3,3,32,32]{3,2,1,0:T(8,128)(2,1)} %wmid_ref.1, bf16[2,32]{1,0:T(2,128)(2,1)} %whead_ref.1), custom_call_target="tpu_custom_call" | custom-call | tf_op jit(solution)/shard_map/pallas_call | solution.py:514
  28.1 2.2 %copy.12 = f32[1,1,1,23,9568]{4,3,2,1,0:T(8,128)} copy(f32[1,1,1,23,9568]{4,2,3,1,0:T(1,128)} %param.13) | data formatting | bytes 1760512
  30.2 0.0 copy-start.1
  30.2 39.4 %shard_map.95 = f32[24,9568]{1,0:T(8,128)} custom-call(f32[23,9568]{1,0:T(8,128)} %bitcast.3, f32[80,128]{1,0:T(8,128)} %get-tuple-element.8.layer_ref), custom_call_target="tpu_custom_call" | custom-call | tf_op jit(solution)/shard_map/pallas_call | solution.py:207
  69.7 0.0 copy-done.1
  69.7 0.0 copy-start
  69.7 0.6 copy.16
  70.3 0.1 copy-done
  70.4 0.6 copy.17
  71.0 2.2 %copy.18 = f32[24,9568]{1,0:T(8,128)} copy(f32[24,9568]{1,0:T(8,128)} %shard_map.95) | data formatting | bytes 1837056
Async XLA Ops:
  30.2 39.4 %copy-start.1 = (f32[1,32,128]{2,1,0:T(8,128)S(1)}, f32[1,32,128]{2,1,0:T(8,128)}, u32[]{:S(2)}) copy-start(f32[1,32,128]{2,1,0:T(8,128)} %get-tuple-element.12) | copy-start | bytes 49156
  69.7 0.7 copy-start

commit v3 on v2

v3 whole, which is shorter than its diff:
```python
import functools
import math

import jax
import jax.numpy as jnp
from jax import lax
from jax.experimental import pallas as pl
from jax.experimental.pallas import tpu as pltpu
from jax.sharding import PartitionSpec as P

MESH = pl.DeviceIdType.MESH
UNITS = 10


def flat_roll(value, offset):
    return pltpu.roll(value, (-offset) % value.shape[-1], value.ndim - 1)


def halves(value):
    high = value.astype(jnp.bfloat16)
    return high, (value - high.astype(jnp.float32)).astype(jnp.bfloat16)


def nt(a, b, **how):
    return lax.dot_general(a, b, (((1,), (1,)), ((), ())), preferred_element_type=jnp.float32, **how)


def dot(a, b):
    return jnp.dot(a, b, preferred_element_type=jnp.float32)


def lanes_of(shape):
    return lax.broadcasted_iota(jnp.int32, shape, len(shape) - 1)


def fused_kernel(scale, field_ref, cot_ref, check_ref, win_ref, wmid_ref, whead_ref, prior_ref,
                 coupled_ref, fgrad_ref, out_ref,
                 near_f, near_c, near_k, ext, pack_out, pack_in, taps, edge_taps, w9, w2, w3,
                 xm, xs_one, xd, xds, cp, pair_rows, t_rows, acc_mid, b_rows,
                 c_own, c_in, xs, xr, zs, zr, fin, wide, mine, mine_in, mine_x, mine_z, own_sum, mine_fin,
                 sem_r, sem_p, sem_own, sem_c, sem_x, sem_z, sem_t, sem_a, sem_b, sem_l, sem_lx, sem_lz, sem_la, sem_lr):
    f32, bf = jnp.float32, jnp.bfloat16
    dp, core, gy = lax.axis_index("dp"), lax.axis_index("gx"), lax.axis_index("gy")
    n_gy = lax.axis_size("gy")
    n_z = lax.axis_size("dp") // 2
    n_p = 2 * n_gy
    z = lax.rem(dp, n_z)
    p = lax.div(dp, n_z) * n_gy + gy
    other = 1 - core
    share = c_own.shape[0]

    def plane(q, which=core):
        return {"dp": lax.div(q, n_gy) * n_z + z, "gx": which, "gy": lax.rem(q, n_gy)}

    def along(w):
        return {"dp": dp - z + w, "gx": core, "gy": gy}

    def chunk(q, rows=64):
        return pl.ds(pl.multiple_of(rows * q, rows), rows)

    partner = {"dp": dp, "gx": other, "gy": gy}
    left = {"dp": dp, "gx": core, "gy": lax.rem(gy + n_gy - 1, n_gy)}
    right = {"dp": dp, "gx": core, "gy": lax.rem(gy + 1, n_gy)}
    barrier = pltpu.get_barrier_semaphore()

    def hello(who):
        pl.semaphore_signal(barrier, inc=1, device_id=who, device_id_type=MESH)

    def hello_along(i, _):
        hello(along(lax.rem(z + i, n_z)))
        return 0

    def hello_plane(i, _):
        hello(plane(lax.rem(p + i, n_p)))
        hello(plane(lax.rem(p + i, n_p), other))
        return 0

    lax.fori_loop(1, n_z, hello_along, 0)
    lax.fori_loop(1, n_p, hello_plane, 0)
    hello(partner)

    def remote(src, dst, sends, recvs, who):
        return pltpu.make_async_remote_copy(src_ref=src, dst_ref=dst, send_sem=sends, recv_sem=recvs, device_id=who, device_id_type=MESH)

    skip = prior_ref.shape[0] - share
    load = pltpu.make_async_copy(prior_ref.at[pl.ds(skip * core, share)], c_own, sem_own)
    load.start()

    def to_plane(q, slot):
        return remote(xs.at[chunk(q)], xr.at[slot], sem_x.at[0, q], sem_x.at[1, slot], plane(q))

    def to_along(w, slot):
        return remote(zs.at[lax.rem(w, 4)], zr.at[slot], sem_z.at[0, w], sem_z.at[1, slot], along(w))

    for a in range(3):
        w9[3 * a : 3 * a + 3, 0:32] = win_ref[a]
    w9[9:16, 0:32] = jnp.zeros((7, 32), f32)
    eye_f = (lax.broadcasted_iota(jnp.int32, (32, 32), 0) == lanes_of((32, 32))).astype(f32)
    eye = eye_f.astype(bf)
    w_taps = w9[:, 0:32]
    taps_t = nt(eye_f, w_taps, precision=lax.Precision.HIGHEST)
    th, tl = halves(taps_t)
    w_one = jnp.concatenate([th, th, tl], axis=1)
    wh, wl = halves(w_taps)
    w_back = jnp.concatenate([wh, wh, wl], axis=1)
    head = whead_ref[...]
    head_t = nt(eye, head)
    head_0, head_1 = head_t[:, 0:1], head_t[:, 1:2]
    for a in range(3):
        for b in range(3):
            k = 3 * a + b
            w2[:, 32 * k : 32 * k + 32] = wmid_ref[a, b]
            kb = 3 * (2 - a) + b
            w3[:, 32 * kb : 32 * kb + 32] = wmid_ref[a, b].astype(f32).T.astype(bf)

    zeros = jnp.zeros((8, 128), f32)
    for i in range(3):
        ext[i, 40:48] = zeros
    ext[0, 4:36] = field_ref[0]
    ext[1, 4:36] = cot_ref[0]
    ext[2, 4:36] = check_ref[...].astype(f32)
    pl.semaphore_wait(barrier, 1 + 2 * (n_p - 1) + (n_z - 1))
    swaps = [
        pltpu.make_async_remote_copy(src_ref=src, dst_ref=dst, send_sem=sem_r.at[0, i], recv_sem=sem_r.at[1, i], device_id=partner, device_id_type=MESH)
        for i, (src, dst) in enumerate(((field_ref, near_f), (cot_ref, near_c), (check_ref, near_k)))
    ]
    for swap in swaps:
        swap.start()
    halves_swap = remote(prior_ref.at[pl.ds(skip * other, share)], c_in, sem_c.at[0], sem_c.at[1], partner)
    halves_swap.start()
    for swap in swaps:
        swap.wait_recv()
    ext[0, 0:4], ext[0, 36:40] = near_f[0, 28:32], near_f[0, 0:4]
    ext[1, 0:4], ext[1, 36:40] = near_c[0, 28:32], near_c[0, 0:4]
    ext[2, 0:4], ext[2, 36:40] = near_k[28:32].astype(f32), near_k[0:4].astype(f32)

    row_16 = lax.broadcasted_iota(jnp.int32, (16, 128), 0)
    lane_16 = lanes_of((16, 128))
    own_lanes = lax.div(lane_16, 8) == row_16
    for i in range(3):
        for t in range(3):
            turned = pltpu.roll(ext[i, 16 * t : 16 * t + 16], 4, 1, stride=8, stride_axis=0)
            pack_out[3 * i + t : 3 * i + t + 1] = jnp.sum(jnp.where(own_lanes, turned, 0.0), axis=0, keepdims=True)
    pack_out[9:16] = jnp.zeros((7, 128), f32)
    posts = [
        pltpu.make_async_remote_copy(src_ref=pack_out, dst_ref=pack_in.at[i], send_sem=sem_p.at[0, i], recv_sem=sem_p.at[1, i], device_id=who, device_id_type=MESH)
        for i, who in ((1, left), (0, right))
    ]
    for post in posts:
        post.start()

    load.wait()
    halves_swap.wait_recv()
    n_cols = prior_ref.shape[2]
    whole = n_cols // 128 * 128

    def pair_sum(r, _):
        at = pl.multiple_of(80 * r, 16)
        for j in range(4):
            cols = slice(2048 * j, 2048 * j + 2048)
            value = c_own[r, :, cols] + c_in[r, :, cols]
            xs[pl.ds(at + 16 * j, 16)] = value.reshape(16, 128).astype(bf)
        value = (c_own[r, :, 8192:whole] + c_in[r, :, 8192:whole]).reshape((whole - 8192) // 128, 128)
        last = c_own[r, :, whole:] + c_in[r, :, whole:]
        last = jnp.concatenate([last, jnp.zeros((1, whole + 128 - n_cols), f32)], axis=1)
        value = jnp.concatenate([value, last, jnp.zeros((16 - 1 - value.shape[0], 128), f32)], axis=0)
        xs[pl.ds(at + 64, 16)] = value.astype(bf)
        return 0

    lax.fori_loop(0, share, pair_sum, 0)
    xs[80 * share :] = jnp.zeros((xs.shape[0] - 80 * share, 128), bf)

    def send_plane(i, _):
        to_plane(lax.rem(p + i, n_p), p).start()
        return 0

    lax.fori_loop(1, n_p, send_plane, 0)

    for post in posts:
        post.wait_recv()
    column = lax.rem(lane_16, 8)
    own = pack_out[...]
    slab_l = jnp.where(column >= 4, own, pack_in[0])
    slab_r = jnp.where(column < 4, own, pack_in[1])

    def flat(slab, i):
        return jnp.concatenate([slab[3 * i + t : 3 * i + t + 1] for t in range(3)], axis=1)

    def flat_both(i):
        return jnp.concatenate([flat(slab_l, i), flat(slab_r, i)], axis=1)

    field_s, cot_s, frozen_s = flat_both(0), flat_both(1), flat_both(2)
    masked_s = field_s * frozen_s

    def both_rolled(value, offset):
        return jnp.concatenate([flat_roll(value[:, :384], offset), flat_roll(value[:, 384:], offset)], axis=1)

    def unflat(vector, e):
        parts = []
        for t in range(3):
            spread = jnp.broadcast_to(vector[:, 128 * t : 128 * t + 128], (16, 128))
            parts.append(jnp.sum(jnp.where(lane_16 == 8 * row_16 + e, spread, 0.0), axis=1, keepdims=True))
        return jnp.concatenate(parts, axis=0)

    masked = ext[0] * ext[2]
    lane_48 = lanes_of((48, 128))
    shifts = (
        jnp.where(lane_48 == 0, unflat(masked_s[:, :384], 3), pltpu.roll(masked, 1, 1)),
        masked,
        jnp.where(lane_48 == 127, unflat(masked_s[:, 384:], 4), pltpu.roll(masked, 127, 1)),
    )
    taps[...] = jnp.zeros(taps.shape, f32)
    edge_taps[...] = jnp.zeros(edge_taps.shape, f32)
    for a in range(3):
        for b in range(3):
            k = 3 * a + b
            taps[pl.ds(16 + k, 38, stride=16), :] = shifts[b][a : a + 38]
            edge_taps[k : k + 1, :] = both_rolled(masked_s, 8 * (a - 1) + b - 1)

    def first(tap_values):
        high, low = halves(tap_values)
        return jnp.tanh(dot(w_one, jnp.concatenate([high, low, high], axis=0))).astype(bf)

    lane_384 = lanes_of((32, 384))

    def spread_edges(value, back, store):
        for a in range(3):
            for b in range(3):
                k = 3 * a + b
                offset = 8 * (a - 1) + (1 - b if back else b - 1)
                store[32 * k : 32 * k + 32, :] = both_rolled(value, offset).astype(bf)
        mixed = jnp.where(lax.rem(lane_384, 8) == 4, flat_roll(value[:, :384], -1), flat_roll(value[:, 384:], 1))
        for t in range(3):
            cp[t] = mixed[:, 128 * t : 128 * t + 128]

    lane_32 = lanes_of((32, 128))

    def spread_row(q, value, back, store):
        edge = pltpu.roll(cp[lax.div(q, 16)], lax.rem(252 - 8 * lax.rem(q, 16), 128), 1)
        before = jnp.where(lane_32 == 0, edge, pltpu.roll(value, 1, 1)).astype(bf)
        after = jnp.where(lane_32 == 127, edge, pltpu.roll(value, 127, 1)).astype(bf)
        store[q, 0:32] = after if back else before
        store[q, 32:64] = value.astype(bf)
        store[q, 64:96] = before if back else after

    one_s = first(edge_taps[...])
    spread_edges(one_s.astype(f32), False, xs_one)

    def one_rows(rows):
        values = jnp.concatenate([taps[pl.ds(pl.multiple_of(16 * q, 16), 16), :] for q in rows], axis=1)
        out = first(values).astype(f32)
        for i, q in enumerate(rows):
            spread_row(q, out[:, 128 * i : 128 * i + 128], False, xm)

    def over_rows(step, first_group=0, last_group=8):
        def body(i, _):
            step([4 + 4 * i + n for n in range(4)])
            return 0

        lax.fori_loop(first_group, last_group, body, 0)

    for q in (0, 39):
        xm[q] = jnp.zeros((96, 128), bf)
    one_rows([1, 2, 3, 36])
    one_rows([37, 38])
    over_rows(one_rows)

    def second(windows, field, cot, frozen):
        two = jnp.tanh(dot(w2[...], windows)).astype(bf)
        pair = dot(head, two)
        expo = jnp.exp(pair[0:1])
        open_cot = (1.0 - frozen) * cot
        d_0 = (open_cot * field * expo).astype(bf)
        d_1 = open_cot.astype(bf)
        two_f = two.astype(f32)
        d_two = (head_0 * d_0.astype(f32) + head_1 * d_1.astype(f32)) * (1.0 - two_f * two_f)
        return two, pair, d_0, d_1, d_two.astype(bf).astype(f32)

    _, _, _, _, d_two_s = second(xs_one[...], field_s, cot_s, frozen_s)
    spread_edges(d_two_s, True, xds)

    def windows_of(store, rows):
        return jnp.concatenate([store[pl.ds(q - 1, 3)].reshape(288, 128) for q in rows], axis=1)

    def rows_of(i, rows):
        return jnp.concatenate([ext[i, pl.ds(q, 1), :] for q in rows], axis=1)

    acc_mid[...] = jnp.zeros(acc_mid.shape, f32)
    b_rows[...] = jnp.zeros(b_rows.shape, f32)

    def two_rows(rows, inner=True):
        two, pair, d_0, d_1, d_two = second(windows_of(xm, rows), rows_of(0, rows), rows_of(1, rows), rows_of(2, rows))
        for i, q in enumerate(rows):
            at = slice(128 * i, 128 * i + 128)
            spread_row(q, d_two[:, at], True, xd)
            if inner:
                pair_rows[pl.ds(pl.multiple_of(8 * q, 8), 2), :] = pair[:, at]
        if inner:
            b_rows[297:299, 0:32] += nt(jnp.concatenate([d_0, d_1], axis=0), two)

    for q in (0, 1, 38, 39):
        xd[q] = jnp.zeros((96, 128), bf)
    two_rows([2, 3, 36, 37], inner=False)
    over_rows(two_rows, 0, 4)
    def take_plane(i, total):
        q = lax.rem(p + n_p - i, n_p)
        to_plane(q, q).wait_recv()
        return total + xr[q].astype(f32)

    total = lax.fori_loop(1, n_p, take_plane, xs[chunk(p)].astype(f32))
    zs[...] = total.astype(bf).reshape(4, 16, 128)

    def send_along(i, _):
        to_along(lax.rem(z + i, n_z), z).start()
        return 0

    lax.fori_loop(1, n_z, send_along, 0)
    over_rows(two_rows, 4, 8)

    def third(windows, one):
        one_f = one.astype(f32)
        d_one = dot(w3[...], windows) * (1.0 - one_f * one_f)
        high, low = halves(d_one)
        return high, low, dot(w_back, jnp.concatenate([high, low, high], axis=0))

    _, _, t_s = third(xds[...], one_s)

    def three_rows(rows, inner=True):
        windows = windows_of(xd, rows)
        one = jnp.concatenate([xm[q, 32:64] for q in rows], axis=1)
        high, low, t_values = third(windows, one)
        for i, q in enumerate(rows):
            t_rows[pl.ds(pl.multiple_of(16 * q, 16), 16), :] = t_values[:, 128 * i : 128 * i + 128]
        if inner:
            acc_mid[...] += nt(windows, one)
            values = jnp.concatenate([taps[pl.ds(pl.multiple_of(16 * q, 16), 16), :] for q in rows], axis=1)
            m_high, m_low = halves(values)
            parts = nt(jnp.concatenate([m_high, m_low], axis=0), jnp.concatenate([high, low], axis=0))
            parts = parts[0:16] + parts[16:32]
            b_rows[0:9, 0:32] += (parts[:, 0:32] + parts[:, 32:64])[0:9]

    three_rows([3, 36], inner=False)
    over_rows(three_rows)

    for j in range(3):
        b_rows[9 + 96 * (2 - j) : 9 + 96 * (2 - j) + 96, 0:32] = acc_mid[96 * j : 96 * j + 96]
    rows = mine.shape[0]
    layer = b_rows[pl.ds(0, rows, stride=4), :]
    for g in range(1, 4):
        layer = layer + pltpu.roll(b_rows[pl.ds(g, rows, stride=4), :], 32 * g, 1)
    mine[...] = layer * scale

    mine_swap = remote(mine, mine_in, sem_l.at[0], sem_l.at[1], partner)
    mine_swap.start()

    def column_sum(b):
        total = None
        for a in range(3):
            part = t_rows[pl.ds(16 * (5 - a) + 3 * a + b, 32, stride=16), :]
            total = part if total is None else total + part
        return total

    def edge_sum(b, side):
        total = None
        for a in range(3):
            k = 3 * a + b
            part = flat_roll(t_s[k : k + 1, 384 * side : 384 * side + 384], 8 * (1 - a))
            total = part if total is None else total + part
        return total

    lane = lanes_of((32, 128))
    from_right = unflat(edge_sum(0, 1), 4)[4:36]
    from_left = unflat(edge_sum(2, 0), 3)[4:36]
    d_masked = (
        jnp.where(lane == 127, from_right, pltpu.roll(column_sum(0), 127, 1))
        + column_sum(1)
        + jnp.where(lane == 0, from_left, pltpu.roll(column_sum(2), 1, 1))
    )
    frozen = check_ref[...].astype(f32)
    unfrozen = 1.0 - frozen
    expo = jnp.exp(pair_rows[pl.ds(32, 32, stride=8), :])
    offset = pair_rows[pl.ds(33, 32, stride=8), :]
    values, cot = field_ref[0], cot_ref[0]
    coupled_ref[0] = frozen * values + unfrozen * (values * expo + offset)
    fgrad_ref[0] = frozen * cot + unfrozen * cot * expo + frozen * d_masked


    mine_swap.wait()
    for i in range(UNITS // 2):
        unit = 2 * i + core
        own_sum[unit] = mine[chunk(unit, 8)] + mine_in[chunk(unit, 8)]

    def to_owner(i, slot):
        unit = 2 * i + core
        return remote(own_sum.at[unit], mine_x.at[slot], sem_lx.at[0, i], sem_lx.at[1, slot], plane(unit))

    for i in range(UNITS // 2):

        @pl.when(2 * i + core != p)
        def _():
            to_owner(i, p).start()

    tile = lax.rem(z, 4)

    def take_along(i, total):
        w = lax.rem(z + n_z - i, n_z)
        to_along(w, w).wait_recv()
        return total + zr[w].astype(f32)

    total = lax.fori_loop(1, n_z, take_along, zs[tile].astype(f32))
    fin[core, chunk(4 * p + tile, 16)] = total.astype(bf)

    def to_four(i, slot):
        w = z - tile + lax.rem(tile + i, 4)
        at = chunk(4 * p + slot, 16)
        return remote(fin.at[core, chunk(4 * p + tile, 16)], fin.at[core, at], sem_t.at[0, i], sem_t.at[1, slot], along(w))

    for i in range(1, 4):
        to_four(i, tile).start()

    is_owner = (p < UNITS) & (lax.rem(p, 2) == core)

    def to_along_mine(w, slot):
        return remote(mine_x.at[p], mine_z.at[slot], sem_lz.at[0, w], sem_lz.at[1, slot], along(w))

    @pl.when(is_owner)
    def _():
        def take(i, total):
            q = lax.rem(p + n_p - i, n_p)
            to_owner(lax.div(p, 2), q).wait_recv()
            return total + mine_x[q]

        mine_x[p] = lax.fori_loop(1, n_p, take, own_sum[p])

        def send(i, _):
            to_along_mine(lax.rem(z + i, n_z), z).start()
            return 0

        lax.fori_loop(1, n_z, send, 0)

    for i in range(1, 4):
        to_four(i, lax.rem(tile + i, 4)).wait_recv()

    def all_plane(q, slot):
        return remote(fin.at[core, chunk(p)], fin.at[core, chunk(slot)], sem_a.at[0, q], sem_a.at[1, slot], plane(q))

    def to_partner(which, slot):
        return remote(fin.at[core, chunk(slot)], fin.at[which, chunk(slot)], sem_b.at[0, slot], sem_b.at[1, slot], partner)

    def send_all(i, _):
        all_plane(lax.rem(p + i, n_p), p).start()
        return 0

    lax.fori_loop(1, n_p, send_all, 0)
    to_partner(core, p).start()

    def take_all(i, _):
        q = lax.rem(p + n_p - i, n_p)
        all_plane(q, q).wait_recv()
        to_partner(core, q).start()
        return 0

    lax.fori_loop(1, n_p, take_all, 0)

    def to_all_mine(q, which, unit):
        return remote(mine_fin.at[unit], mine_fin.at[unit], sem_la.at[which, q], sem_lr.at[unit], plane(q, which))

    @pl.when(is_owner)
    def _():
        def take(i, total):
            w = lax.rem(z + n_z - i, n_z)
            to_along_mine(w, w).wait_recv()
            return total + mine_z[w]

        mine_fin[p] = lax.fori_loop(1, n_z, take, mine_x[p])

        def send(i, _):
            q = lax.rem(p + i, n_p)
            to_all_mine(q, core, p).start()
            to_all_mine(q, other, p).start()
            return 0

        lax.fori_loop(1, n_p, send, 0)
        to_all_mine(p, other, p).start()

    base = 80 * (1 + skip * core)
    for_other = 80 * (1 + skip * other)
    used = 80 * share // 64

    def widen(q, _):
        wide[pl.ds(pl.multiple_of(base + 64 * q, 16), 64)] = fin[core, chunk(q)].astype(f32)
        return 0

    def widen_other(q, _):
        to_partner(other, q).wait_recv()
        wide[pl.ds(pl.multiple_of(for_other + 64 * q, 16), 64)] = fin[other, chunk(q)].astype(f32)
        return 0

    lax.fori_loop(0, used, widen, 0)
    lax.fori_loop(0, used, widen_other, 0)
    for q in range(used, n_p):
        to_partner(other, q).wait_recv()

    for unit in range(UNITS):

        @pl.when((p != unit) | (core != unit % 2))
        def _():
            to_all_mine(p, other, unit).wait_recv()

        wide[8 * unit : 8 * unit + 8] = mine_fin[unit]

    def unpack(k, _):
        out_ref[:, pl.ds(pl.multiple_of(k * 128, 128), 128)] = wide[pl.ds(k, 24, stride=80), :]
        return 0

    lax.fori_loop(0, whole // 128, unpack, 0)
    out_ref[:, whole:] = wide[pl.ds(whole // 128, 24, stride=80), :][:, : n_cols - whole]

    for copy in (*swaps, *posts, halves_swap):
        copy.wait_send()

    def drain_plane(i, _):
        q = lax.rem(p + i, n_p)
        to_plane(q, p).wait_send()
        all_plane(q, p).wait_send()
        return 0

    def drain_along(i, _):
        to_along(lax.rem(z + i, n_z), z).wait_send()
        return 0

    def drain_partner(q, _):
        to_partner(core, q).wait_send()
        return 0

    lax.fori_loop(1, n_p, drain_plane, 0)
    lax.fori_loop(1, n_z, drain_along, 0)
    lax.fori_loop(0, n_p, drain_partner, 0)
    for i in range(1, 4):
        to_four(i, tile).wait_send()
    for i in range(UNITS // 2):

        @pl.when(2 * i + core != p)
        def _():
            to_owner(i, p).wait_send()

    @pl.when(is_owner)
    def _():
        def drain_z(i, _):
            to_along_mine(lax.rem(z + i, n_z), z).wait_send()
            return 0

        def drain_all(i, _):
            q = lax.rem(p + i, n_p)
            to_all_mine(q, core, p).wait_send()
            to_all_mine(q, other, p).wait_send()
            return 0

        lax.fori_loop(1, n_z, drain_z, 0)
        lax.fori_loop(1, n_p, drain_all, 0)
        to_all_mine(p, other, p).wait_send()


def fused_call(scale, field, cot, checker, weight_in, weight_mid, weight_head, prior):
    f32, bf = jnp.float32, jnp.bfloat16
    sem = pltpu.SemaphoreType.DMA
    vmem = pl.BlockSpec(memory_space=pltpu.VMEM)
    n_p, n_z = 2 * lax.axis_size("gy"), lax.axis_size("dp") // 2
    rows, _, cols = prior.shape
    share = (rows + 1) // 2
    return pl.pallas_call(
        functools.partial(fused_kernel, scale),
        out_shape=(
            jax.ShapeDtypeStruct(field.shape, f32),
            jax.ShapeDtypeStruct(field.shape, f32),
            jax.ShapeDtypeStruct((rows + 1, cols), f32),
        ),
        in_specs=[vmem] * 6 + [pl.BlockSpec(memory_space=pl.ANY)],
        out_specs=(vmem,) * 3,
        scratch_shapes=[
            pltpu.VMEM(field.shape, f32), pltpu.VMEM(field.shape, f32), pltpu.VMEM(checker.shape, jnp.int32),
            pltpu.VMEM((3, 48, 128), f32),
            pltpu.VMEM((16, 128), f32), pltpu.VMEM((2, 16, 128), f32),
            pltpu.VMEM((640, 128), f32), pltpu.VMEM((16, 768), f32),
            pltpu.VMEM((16, 128), f32), pltpu.VMEM((32, 288), bf), pltpu.VMEM((32, 288), bf),
            pltpu.VMEM((40, 96, 128), bf), pltpu.VMEM((288, 768), bf),
            pltpu.VMEM((40, 96, 128), bf), pltpu.VMEM((288, 768), bf),
            pltpu.VMEM((3, 32, 128), f32),
            pltpu.VMEM((320, 128), f32), pltpu.VMEM((640, 128), f32),
            pltpu.VMEM((288, 32), f32), pltpu.VMEM((320, 128), f32),
            pltpu.VMEM((share, 1, cols), f32), pltpu.VMEM((share, 1, cols), f32),
            pltpu.VMEM((n_p * 64, 128), bf), pltpu.VMEM((n_p, 64, 128), bf),
            pltpu.VMEM((4, 16, 128), bf), pltpu.VMEM((n_z, 16, 128), bf),
            pltpu.VMEM((2, n_p * 64, 128), bf), pltpu.VMEM((80 * (rows + 1), 128), f32),
            pltpu.VMEM((80, 128), f32), pltpu.VMEM((80, 128), f32),
            pltpu.VMEM((n_p, 8, 128), f32), pltpu.VMEM((n_z, 8, 128), f32),
            pltpu.VMEM((UNITS, 8, 128), f32), pltpu.VMEM((UNITS, 8, 128), f32),
            sem((2, 3)), sem((2, 2)), sem, sem((2,)), sem((2, n_p)), sem((2, n_z)), sem((2, 4)), sem((2, n_p)), sem((2, n_p)),
            sem((2,)), sem((2, n_p)), sem((2, n_z)), sem((2, n_p)), sem((UNITS,)),
        ],
        compiler_params=pltpu.CompilerParams(collective_id=0, has_side_effects=True),
    )(field, cot, checker, weight_in, weight_mid, weight_head, prior)


def on_device(field, cotangent, checker, weight_in, weight_mid, weight_head, prior_grads):
    cell_total = field.size * lax.axis_size("dp") * lax.axis_size("gx") * lax.axis_size("gy")
    scale = 1.0 / math.sqrt(cell_total)
    prior = prior_grads.reshape(prior_grads.shape[3], 1, prior_grads.shape[4])
    return fused_call(scale, field, cotangent, checker, weight_in, weight_mid, weight_head, prior)


def solution(mesh):
    placed = (
        P("dp", "gx", "gy"),
        P("dp", "gx", "gy"),
        P("gx", "gy"),
        P(),
        P(),
        P(),
        P("dp", "gx", "gy", None, None),
    )
    return jax.shard_map(
        on_device,
        mesh=mesh,
        in_specs=placed,
        out_specs=(P("dp", "gx", "gy"), P("dp", "gx", "gy"), P()),
        check_vma=False,
    )
```

time: 73.5 us -> 59.7 us (0.81)
  Pallas kernels: 66.8 us -> 54.7 us
  local copies, waits for them, and re-layouts: 5.64 us -> 4.1 us
    pallas_call x2 -> x1, Pallas kernels: 66.8 us -> 54.7 us  [fused_call(): pl.pallas_call(functools.partial(fused_kernel, scale), out_shape=(jax.Sha...]
    unnamed x8 -> x5, local copies, waits for them, and re-layouts: 5.64 us -> 4.1 us
where the time goes in v3:
time: 59.7 us; the launch traced here: 59.4 us
  Pallas kernels  54.7 us (92%)
  local copies, waits for them, and re-layouts  4.1 us (7%)
  between operations  0.65 us (1%)
    pallas_call x1, Pallas kernels, fused_call(): pl.pallas_call(functools.partial(fused_kernel, scale), out_shape=(jax.Sha...  54.7 us
    unnamed x5, local copies, waits for them, and re-layouts  4.1 us

profile of v3, /device:TPU:1, one launch (start us, length us, event | category | flops | bytes accessed | tf_op | source)
XLA Modules:
  0.0 59.4 jit_solution(15398231204391531827)
XLA Ops:
  0.6 54.7 %shard_map.94 = (f32[1,32,128]{2,1,0:T(8,128)}, f32[1,32,128]{2,1,0:T(8,128)}, f32[24,9568]{1,0:T(8,128)}) custom-call(f32[1,32,128]{2,1,0:T(8,128)} %field_ref.1, f32[1,32,128]{2,1,0:T(8,128)} %cot_ref.1, s32[32,128]{1,0:T(8,128)} %check_ref.1, f32[3,3,32]{2,1,0:T(4,128)} %win_ref.1, bf16[3,3,32,32]{3,2,1,0:T(8,128)(2,1)} %wmid_ref.1, ...), custom_call_target="tpu_custom_call" | custom-call | tf_op jit(solution)/shard_map/pallas_call | solution.py:571
  55.3 0.0 copy-start
  55.3 1.3 %copy.13 = f32[1,32,128]{2,1,0:T(8,128)} copy(f32[1,32,128]{2,1,0:T(8,128)} %get-tuple-element.6) | data formatting | bytes 32768
  56.6 0.0 copy-done
  56.6 0.6 %copy.14 = f32[1,32,128]{2,1,0:T(8,128)} copy(f32[1,32,128]{2,1,0:T(8,128)S(1)} %copy-done) | data formatting | bytes 32768
  57.3 2.2 %copy.15 = f32[24,9568]{1,0:T(8,128)} copy(f32[24,9568]{1,0:T(8,128)} %get-tuple-element.8) | data formatting | bytes 1837056
Async XLA Ops:
  55.3 1.3 %copy-start = (f32[1,32,128]{2,1,0:T(8,128)S(1)}, f32[1,32,128]{2,1,0:T(8,128)}, u32[]{:S(2)}) copy-start(f32[1,32,128]{2,1,0:T(8,128)} %get-tuple-element.7) | copy-start | bytes 49156

commit v4 on v3

--- a/solution.py
+++ b/solution.py
@@ -1,4 +1,5 @@
 import functools
+import itertools
 import math
 
 import jax
@@ -12,6 +13,15 @@
 UNITS = 10
 
 
+def ring_distance(offset, size):
+    return min(offset, size - offset)
+
+
+def farthest_first(*sizes):
+    offsets = [at for at in itertools.product(*(range(n) for n in sizes)) if any(at)]
+    return sorted(offsets, key=lambda at: -sum(ring_distance(o, n) for o, n in zip(at, sizes)))
+
+
 def flat_roll(value, offset):
     return pltpu.roll(value, (-offset) % value.shape[-1], value.ndim - 1)
 
@@ -34,10 +44,10 @@
 
 
 def fused_kernel(scale, field_ref, cot_ref, check_ref, win_ref, wmid_ref, whead_ref, prior_ref,
-                 coupled_ref, fgrad_ref, out_ref,
+                 coupled_ref, fgrad_ref, fin, mine_fin,
                  near_f, near_c, near_k, ext, pack_out, pack_in, taps, edge_taps, w9, w2, w3,
                  xm, xs_one, xd, xds, cp, pair_rows, t_rows, acc_mid, b_rows,
-                 c_own, c_in, xs, xr, zs, zr, fin, wide, mine, mine_in, mine_x, mine_z, own_sum, mine_fin,
+                 c_own, c_in, xs, xr, zs, zr, mine, mine_x, mine_z, own_sum,
                  sem_r, sem_p, sem_own, sem_c, sem_x, sem_z, sem_t, sem_a, sem_b, sem_l, sem_lx, sem_lz, sem_la, sem_lr):
     f32, bf = jnp.float32, jnp.bfloat16
     dp, core, gy = lax.axis_index("dp"), lax.axis_index("gx"), lax.axis_index("gy")
@@ -48,6 +58,18 @@
     p = lax.div(dp, n_z) * n_gy + gy
     other = 1 - core
     share = c_own.shape[0]
+
+    n_x, n_y = n_gy // 2, 4
+    at_x, at_y = lax.div(gy, 2), 2 * lax.rem(gy, 2) + lax.div(dp, n_z)
+    plane_order = farthest_first(n_x, n_y)
+    line_order = [w for (w,) in farthest_first(n_z)]
+
+    def beside(dx, dy):
+        to_x, to_y = lax.rem(at_x + dx, n_x), lax.rem(at_y + dy, n_y)
+        return lax.rem(to_y, 2) * n_gy + 2 * to_x + lax.div(to_y, 2)
+
+    def from_beside(dx, dy):
+        return beside(n_x - dx, n_y - dy)
 
     def plane(q, which=core):
         return {"dp": lax.div(q, n_gy) * n_z + z, "gx": which, "gy": lax.rem(q, n_gy)}
@@ -170,11 +192,8 @@
     lax.fori_loop(0, share, pair_sum, 0)
     xs[80 * share :] = jnp.zeros((xs.shape[0] - 80 * share, 128), bf)
 
-    def send_plane(i, _):
-        to_plane(lax.rem(p + i, n_p), p).start()
-        return 0
-
-    lax.fori_loop(1, n_p, send_plane, 0)
+    for offset in plane_order:
+        to_plane(beside(*offset), p).start()
 
     for post in posts:
         post.wait_recv()
@@ -302,19 +321,15 @@
         xd[q] = jnp.zeros((96, 128), bf)
     two_rows([2, 3, 36, 37], inner=False)
     over_rows(two_rows, 0, 4)
-    def take_plane(i, total):
-        q = lax.rem(p + n_p - i, n_p)
+    total = xs[chunk(p)].astype(f32)
+    for offset in plane_order:
+        q = from_beside(*offset)
         to_plane(q, q).wait_recv()
-        return total + xr[q].astype(f32)
-
-    total = lax.fori_loop(1, n_p, take_plane, xs[chunk(p)].astype(f32))
+        total = total + xr[q].astype(f32)
     zs[...] = total.astype(bf).reshape(4, 16, 128)
 
-    def send_along(i, _):
-        to_along(lax.rem(z + i, n_z), z).start()
-        return 0
-
-    lax.fori_loop(1, n_z, send_along, 0)
+    for offset in line_order:
+        to_along(lax.rem(z + offset, n_z), z).start()
     over_rows(two_rows, 4, 8)
 
     def third(windows, one):
@@ -350,8 +365,19 @@
         layer = layer + pltpu.roll(b_rows[pl.ds(g, rows, stride=4), :], 32 * g, 1)
     mine[...] = layer * scale
 
-    mine_swap = remote(mine, mine_in, sem_l.at[0], sem_l.at[1], partner)
-    mine_swap.start()
+    is_owner = (p < UNITS) & (lax.rem(p, 2) == core)
+
+    def to_owner(unit, slot):
+        return remote(mine.at[pl.ds(8 * unit, 8)], mine_x.at[slot], sem_l.at[unit], sem_lx.at[slot], plane(unit, unit % 2))
+
+    def is_other(unit):
+        return (p != unit) | (core != unit % 2)
+
+    for unit in range(UNITS):
+
+        @pl.when(is_other(unit))
+        def _():
+            to_owner(unit, n_p * core + p).start()
 
     def column_sum(b):
         total = None
@@ -385,29 +411,13 @@
     fgrad_ref[0] = frozen * cot + unfrozen * cot * expo + frozen * d_masked
 
 
-    mine_swap.wait()
-    for i in range(UNITS // 2):
-        unit = 2 * i + core
-        own_sum[unit] = mine[chunk(unit, 8)] + mine_in[chunk(unit, 8)]
-
-    def to_owner(i, slot):
-        unit = 2 * i + core
-        return remote(own_sum.at[unit], mine_x.at[slot], sem_lx.at[0, i], sem_lx.at[1, slot], plane(unit))
-
-    for i in range(UNITS // 2):
-
-        @pl.when(2 * i + core != p)
-        def _():
-            to_owner(i, p).start()
-
     tile = lax.rem(z, 4)
 
-    def take_along(i, total):
-        w = lax.rem(z + n_z - i, n_z)
+    total = zs[tile].astype(f32)
+    for offset in line_order:
+        w = lax.rem(z + n_z - offset, n_z)
         to_along(w, w).wait_recv()
-        return total + zr[w].astype(f32)
-
-    total = lax.fori_loop(1, n_z, take_along, zs[tile].astype(f32))
+        total = total + zr[w].astype(f32)
     fin[core, chunk(4 * p + tile, 16)] = total.astype(bf)
 
     def to_four(i, slot):
@@ -418,25 +428,19 @@
     for i in range(1, 4):
         to_four(i, tile).start()
 
-    is_owner = (p < UNITS) & (lax.rem(p, 2) == core)
-
     def to_along_mine(w, slot):
-        return remote(mine_x.at[p], mine_z.at[slot], sem_lz.at[0, w], sem_lz.at[1, slot], along(w))
+        return remote(own_sum, mine_z.at[slot], sem_lz.at[0, w], sem_lz.at[1, slot], along(w))
 
     @pl.when(is_owner)
     def _():
         def take(i, total):
-            q = lax.rem(p + n_p - i, n_p)
-            to_owner(lax.div(p, 2), q).wait_recv()
-            return total + mine_x[q]
-
-        mine_x[p] = lax.fori_loop(1, n_p, take, own_sum[p])
-
-        def send(i, _):
-            to_along_mine(lax.rem(z + i, n_z), z).start()
-            return 0
-
-        lax.fori_loop(1, n_z, send, 0)
+            slot = lax.rem(n_p * core + p + i, 2 * n_p)
+            to_owner(0, slot).wait_recv()
+            return total + mine_x[slot]
+
+        own_sum[...] = lax.fori_loop(1, 2 * n_p, take, mine[chunk(p, 8)])
+        for offset in line_order:
+            to_along_mine(lax.rem(z + offset, n_z), z).start()
 
     for i in range(1, 4):
         to_four(i, lax.rem(tile + i, 4)).wait_recv()
@@ -447,20 +451,13 @@
     def to_partner(which, slot):
         return remote(fin.at[core, chunk(slot)], fin.at[which, chunk(slot)], sem_b.at[0, slot], sem_b.at[1, slot], partner)
 
-    def send_all(i, _):
-        all_plane(lax.rem(p + i, n_p), p).start()
-        return 0
-
-    lax.fori_loop(1, n_p, send_all, 0)
+    for offset in plane_order:
+        all_plane(beside(*offset), p).start()
     to_partner(core, p).start()
-
-    def take_all(i, _):
-        q = lax.rem(p + n_p - i, n_p)
+    for offset in plane_order:
+        q = from_beside(*offset)
         all_plane(q, q).wait_recv()
         to_partner(core, q).start()
-        return 0
-
-    lax.fori_loop(1, n_p, take_all, 0)
 
     def to_all_mine(q, which, unit):
         return remote(mine_fin.at[unit], mine_fin.at[unit], sem_la.at[which, q], sem_lr.at[unit], plane(q, which))
@@ -472,49 +469,19 @@
             to_along_mine(w, w).wait_recv()
             return total + mine_z[w]
 
-        mine_fin[p] = lax.fori_loop(1, n_z, take, mine_x[p])
-
-        def send(i, _):
-            q = lax.rem(p + i, n_p)
-            to_all_mine(q, core, p).start()
-            to_all_mine(q, other, p).start()
-            return 0
-
-        lax.fori_loop(1, n_p, send, 0)
+        mine_fin[p] = lax.fori_loop(1, n_z, take, own_sum[...])
+        for offset in plane_order:
+            to_all_mine(beside(*offset), core, p).start()
+            to_all_mine(beside(*offset), other, p).start()
         to_all_mine(p, other, p).start()
 
-    base = 80 * (1 + skip * core)
-    for_other = 80 * (1 + skip * other)
-    used = 80 * share // 64
-
-    def widen(q, _):
-        wide[pl.ds(pl.multiple_of(base + 64 * q, 16), 64)] = fin[core, chunk(q)].astype(f32)
-        return 0
-
-    def widen_other(q, _):
+    for q in range(n_p):
         to_partner(other, q).wait_recv()
-        wide[pl.ds(pl.multiple_of(for_other + 64 * q, 16), 64)] = fin[other, chunk(q)].astype(f32)
-        return 0
-
-    lax.fori_loop(0, used, widen, 0)
-    lax.fori_loop(0, used, widen_other, 0)
-    for q in range(used, n_p):
-        to_partner(other, q).wait_recv()
-
     for unit in range(UNITS):
 
-        @pl.when((p != unit) | (core != unit % 2))
+        @pl.when(is_other(unit))
         def _():
             to_all_mine(p, other, unit).wait_recv()
-
-        wide[8 * unit : 8 * unit + 8] = mine_fin[unit]
-
-    def unpack(k, _):
-        out_ref[:, pl.ds(pl.multiple_of(k * 128, 128), 128)] = wide[pl.ds(k, 24, stride=80), :]
-        return 0
-
-    lax.fori_loop(0, whole // 128, unpack, 0)
-    out_ref[:, whole:] = wide[pl.ds(whole // 128, 24, stride=80), :][:, : n_cols - whole]
 
     for copy in (*swaps, *posts, halves_swap):
         copy.wait_send()
@@ -538,11 +505,11 @@
     lax.fori_loop(0, n_p, drain_partner, 0)
     for i in range(1, 4):
         to_four(i, tile).wait_send()
-    for i in range(UNITS // 2):
-
-        @pl.when(2 * i + core != p)
+    for unit in range(UNITS):
+
+        @pl.when(is_other(unit))
         def _():
-            to_owner(i, p).wait_send()
+            to_owner(unit, n_p * core + p).wait_send()
 
     @pl.when(is_owner)
     def _():
@@ -559,6 +526,48 @@
         lax.fori_loop(1, n_z, drain_z, 0)
         lax.fori_loop(1, n_p, drain_all, 0)
         to_all_mine(p, other, p).wait_send()
+
+
+def unpack_kernel(coupled_in, fgrad_in, fin, mine_fin, coupled_ref, fgrad_ref, out_ref, wide):
+    coupled_ref[...] = coupled_in[...]
+    fgrad_ref[...] = fgrad_in[...]
+    n_rows, n_cols = out_ref.shape
+    share = n_rows // 2
+    for unit in range(UNITS):
+        wide[8 * unit : 8 * unit + 8] = mine_fin[unit]
+    for which in range(2):
+        base = 80 * (1 + (n_rows - 1 - share) * which)
+
+        def widen(r, _):
+            rows = fin[which, pl.ds(pl.multiple_of(80 * r, 16), 80)].astype(jnp.float32)
+            wide[pl.ds(pl.multiple_of(base + 80 * r, 16), 80)] = rows
+            return 0
+
+        lax.fori_loop(0, share, widen, 0, unroll=2)
+
+    def unpack(k, _):
+        out_ref[:, pl.ds(pl.multiple_of(k * 128, 128), 128)] = wide[pl.ds(k, n_rows, stride=80), :]
+        return 0
+
+    whole = n_cols // 128
+    lax.fori_loop(0, whole, unpack, 0, unroll=2)
+    out_ref[:, 128 * whole :] = wide[pl.ds(whole, n_rows, stride=80), :][:, : n_cols - 128 * whole]
+
+
+def unpack_call(coupled, fgrad, fin, mine_fin, rows, cols):
+    f32 = jnp.float32
+    vmem = pl.BlockSpec(memory_space=pltpu.VMEM)
+    return pl.pallas_call(
+        unpack_kernel,
+        out_shape=(
+            jax.ShapeDtypeStruct(coupled.shape, f32),
+            jax.ShapeDtypeStruct(fgrad.shape, f32),
+            jax.ShapeDtypeStruct((rows, cols), f32),
+        ),
+        in_specs=[vmem] * 4,
+        out_specs=(vmem,) * 3,
+        scratch_shapes=[pltpu.VMEM((80 * rows, 128), f32)],
+    )(coupled, fgrad, fin, mine_fin)
 
 
 def fused_call(scale, field, cot, checker, weight_in, weight_mid, weight_head, prior):
@@ -573,10 +582,11 @@
         out_shape=(
             jax.ShapeDtypeStruct(field.shape, f32),
             jax.ShapeDtypeStruct(field.shape, f32),
-            jax.ShapeDtypeStruct((rows + 1, cols), f32),
+            jax.ShapeDtypeStruct((2, n_p * 64, 128), bf),
+            jax.ShapeDtypeStruct((UNITS, 8, 128), f32),
         ),
         in_specs=[vmem] * 6 + [pl.BlockSpec(memory_space=pl.ANY)],
-        out_specs=(vmem,) * 3,
+        out_specs=(vmem,) * 4,
         scratch_shapes=[
             pltpu.VMEM(field.shape, f32), pltpu.VMEM(field.shape, f32), pltpu.VMEM(checker.shape, jnp.int32),
             pltpu.VMEM((3, 48, 128), f32),
@@ -591,12 +601,11 @@
             pltpu.VMEM((share, 1, cols), f32), pltpu.VMEM((share, 1, cols), f32),
             pltpu.VMEM((n_p * 64, 128), bf), pltpu.VMEM((n_p, 64, 128), bf),
             pltpu.VMEM((4, 16, 128), bf), pltpu.VMEM((n_z, 16, 128), bf),
-            pltpu.VMEM((2, n_p * 64, 128), bf), pltpu.VMEM((80 * (rows + 1), 128), f32),
-            pltpu.VMEM((80, 128), f32), pltpu.VMEM((80, 128), f32),
-            pltpu.VMEM((n_p, 8, 128), f32), pltpu.VMEM((n_z, 8, 128), f32),
-            pltpu.VMEM((UNITS, 8, 128), f32), pltpu.VMEM((UNITS, 8, 128), f32),
+            pltpu.VMEM((80, 128), f32),
+            pltpu.VMEM((2 * n_p, 8, 128), f32), pltpu.VMEM((n_z, 8, 128), f32),
+            pltpu.VMEM((8, 128), f32),
             sem((2, 3)), sem((2, 2)), sem, sem((2,)), sem((2, n_p)), sem((2, n_z)), sem((2, 4)), sem((2, n_p)), sem((2, n_p)),
-            sem((2,)), sem((2, n_p)), sem((2, n_z)), sem((2, n_p)), sem((UNITS,)),
+            sem((UNITS,)), sem((2 * n_p,)), sem((2, n_z)), sem((2, n_p)), sem((UNITS,)),
         ],
         compiler_params=pltpu.CompilerParams(collective_id=0, has_side_effects=True),
     )(field, cot, checker, weight_in, weight_mid, weight_head, prior)
@@ -606,7 +615,8 @@
     cell_total = field.size * lax.axis_size("dp") * lax.axis_size("gx") * lax.axis_size("gy")
     scale = 1.0 / math.sqrt(cell_total)
     prior = prior_grads.reshape(prior_grads.shape[3], 1, prior_grads.shape[4])
-    return fused_call(scale, field, cotangent, checker, weight_in, weight_mid, weight_head, prior)
+    sums = fused_call(scale, field, cotangent, checker, weight_in, weight_mid, weight_head, prior)
+    return unpack_call(*sums, prior.shape[0] + 1, prior.shape[2])
 
 
 def solution(mesh):

time: 59.7 us -> 56.5 us (0.946)
  local copies, waits for them, and re-layouts: 4.1 us -> 0 us
  Pallas kernels: 54.7 us -> 55.7 us
    unnamed x5 -> x0, local copies, waits for them, and re-layouts: 4.1 us -> none
    pallas_call x0 -> x1, Pallas kernels: none -> 2.62 us  [unpack_call(): pl.pallas_call(unpack_kernel, out_shape=(jax.ShapeDtypeStruct(coupled.sha...]
    pallas_call x1, Pallas kernels: 54.7 us -> 53 us  [fused_call(): pl.pallas_call(functools.partial(fused_kernel, scale), out_shape=(jax.Sha...]
where the time goes in v4:
time: 56.5 us; the launch traced here: 56.3 us
  Pallas kernels  55.7 us (99%)
  between operations  0.64 us (1%)
    pallas_call x1, Pallas kernels, fused_call(): pl.pallas_call(functools.partial(fused_kernel, scale), out_shape=(jax.Sha...  53 us
    pallas_call x1, Pallas kernels, unpack_call(): pl.pallas_call(unpack_kernel, out_shape=(jax.ShapeDtypeStruct(coupled.sha...  2.62 us

profile of v4, /device:TPU:1, one launch (start us, length us, event | category | flops | bytes accessed | tf_op | source)
XLA Modules:
  0.0 56.3 jit_solution(5761873705156433136)
XLA Ops:
  0.6 53.0 %shard_map.94 = (f32[1,32,128]{2,1,0:T(8,128)}, f32[1,32,128]{2,1,0:T(8,128)}, bf16[2,1024,128]{2,1,0:T(8,128)(2,1)}, f32[10,8,128]{2,1,0:T(8,128)}) custom-call(f32[1,32,128]{2,1,0:T(8,128)} %field_ref.1, f32[1,32,128]{2,1,0:T(8,128)} %cot_ref.1, s32[32,128]{1,0:T(8,128)} %check_ref.1, f32[3,3,32]{2,1,0:T(4,128)} %win_ref.1, ...), custom_call_target="tpu_custom_call" | custom-call | tf_op jit(solution)/shard_map/pallas_call | solution.py:580
  53.7 2.6 %shard_map.95 = (f32[1,32,128]{2,1,0:T(8,128)}, f32[1,32,128]{2,1,0:T(8,128)}, f32[24,9568]{1,0:T(8,128)}) custom-call(f32[1,32,128]{2,1,0:T(8,128)} %get-tuple-element.7.coupled_in, f32[1,32,128]{2,1,0:T(8,128)} %get-tuple-element.8.fgrad_in, bf16[2,1024,128]{2,1,0:T(8,128)(2,1)} %get-tuple-element.9.fin, f32[10,8,128]{2,1,0:T(8,128)} %get-tuple-element.10.mine_fin), custom_call_target="tpu_custom_call" | custom-call | tf_op jit(solution)/shard_map/pallas_call | solution.py:560

commit v5 on v4

--- a/solution.py
+++ b/solution.py
@@ -10,6 +10,7 @@
 from jax.sharding import PartitionSpec as P
 
 MESH = pl.DeviceIdType.MESH
+PIECES = 3
 UNITS = 10
 
 
@@ -44,11 +45,11 @@
 
 
 def fused_kernel(scale, field_ref, cot_ref, check_ref, win_ref, wmid_ref, whead_ref, prior_ref,
-                 coupled_ref, fgrad_ref, fin, mine_fin,
+                 coupled_ref, fgrad_ref, fin, mine_fin, late_fin,
                  near_f, near_c, near_k, ext, pack_out, pack_in, taps, edge_taps, w9, w2, w3,
                  xm, xs_one, xd, xds, cp, pair_rows, t_rows, acc_mid, b_rows,
-                 c_own, c_in, xs, xr, zs, zr, mine, mine_x, mine_z, own_sum,
-                 sem_r, sem_p, sem_own, sem_c, sem_x, sem_z, sem_t, sem_a, sem_b, sem_l, sem_lx, sem_lz, sem_la, sem_lr):
+                 c_own, c_in, xs, xr, zs, zr, mine, mine_x, mine_z, own_sum, b_in, late_x, late_z,
+                 sem_r, sem_p, sem_own, sem_c, sem_x, sem_z, sem_t, sem_a, sem_b, sem_l, sem_lx, sem_lz, sem_la, sem_mr, sem_ls, sem_lr, sem_lt):
     f32, bf = jnp.float32, jnp.bfloat16
     dp, core, gy = lax.axis_index("dp"), lax.axis_index("gx"), lax.axis_index("gy")
     n_gy = lax.axis_size("gy")
@@ -141,6 +142,14 @@
     ext[0, 4:36] = field_ref[0]
     ext[1, 4:36] = cot_ref[0]
     ext[2, 4:36] = check_ref[...].astype(f32)
+    row_16 = lax.broadcasted_iota(jnp.int32, (16, 128), 0)
+    lane_16 = lanes_of((16, 128))
+    own_lanes = lax.div(lane_16, 8) == row_16
+    for i in range(3):
+        for t in range(2):
+            turned = pltpu.roll(ext[i, 4 + 16 * t : 20 + 16 * t], 4, 1, stride=8, stride_axis=0)
+            pack_out[2 * i + t : 2 * i + t + 1] = jnp.sum(jnp.where(own_lanes, turned, 0.0), axis=0, keepdims=True)
+    pack_out[6:8] = jnp.zeros((2, 128), f32)
     pl.semaphore_wait(barrier, 1 + 2 * (n_p - 1) + (n_z - 1))
     swaps = [
         pltpu.make_async_remote_copy(src_ref=src, dst_ref=dst, send_sem=sem_r.at[0, i], recv_sem=sem_r.at[1, i], device_id=partner, device_id_type=MESH)
@@ -148,31 +157,29 @@
     ]
     for swap in swaps:
         swap.start()
-    halves_swap = remote(prior_ref.at[pl.ds(skip * other, share)], c_in, sem_c.at[0], sem_c.at[1], partner)
-    halves_swap.start()
+    posts = [
+        remote(pack_out, pack_in.at[slot], sem_p.at[0, slot], sem_p.at[1, slot], who)
+        for slot, who in (
+            (1, left), (0, right), (3, {**left, "gx": other}), (2, {**right, "gx": other}), (4, partner),
+        )
+    ]
+    for post in posts:
+        post.start()
+    piece = share // PIECES
+    pieces = [
+        remote(prior_ref.at[pl.ds(skip * other + piece * k, piece)], c_in.at[pl.ds(piece * k, piece)], sem_c.at[0, k], sem_c.at[1, k], partner)
+        for k in range(PIECES)
+    ]
+    for copy in pieces:
+        copy.start()
     for swap in swaps:
         swap.wait_recv()
     ext[0, 0:4], ext[0, 36:40] = near_f[0, 28:32], near_f[0, 0:4]
     ext[1, 0:4], ext[1, 36:40] = near_c[0, 28:32], near_c[0, 0:4]
     ext[2, 0:4], ext[2, 36:40] = near_k[28:32].astype(f32), near_k[0:4].astype(f32)
 
-    row_16 = lax.broadcasted_iota(jnp.int32, (16, 128), 0)
-    lane_16 = lanes_of((16, 128))
-    own_lanes = lax.div(lane_16, 8) == row_16
-    for i in range(3):
-        for t in range(3):
-            turned = pltpu.roll(ext[i, 16 * t : 16 * t + 16], 4, 1, stride=8, stride_axis=0)
-            pack_out[3 * i + t : 3 * i + t + 1] = jnp.sum(jnp.where(own_lanes, turned, 0.0), axis=0, keepdims=True)
-    pack_out[9:16] = jnp.zeros((7, 128), f32)
-    posts = [
-        pltpu.make_async_remote_copy(src_ref=pack_out, dst_ref=pack_in.at[i], send_sem=sem_p.at[0, i], recv_sem=sem_p.at[1, i], device_id=who, device_id_type=MESH)
-        for i, who in ((1, left), (0, right))
-    ]
-    for post in posts:
-        post.start()
 
     load.wait()
-    halves_swap.wait_recv()
     n_cols = prior_ref.shape[2]
     whole = n_cols // 128 * 128
 
@@ -189,24 +196,41 @@
         xs[pl.ds(at + 64, 16)] = value.astype(bf)
         return 0
 
-    lax.fori_loop(0, share, pair_sum, 0)
     xs[80 * share :] = jnp.zeros((xs.shape[0] - 80 * share, 128), bf)
-
-    for offset in plane_order:
-        to_plane(beside(*offset), p).start()
+    chunks = 80 * piece // 64
+
+    def reduce_piece(k):
+        pieces[k].wait_recv()
+        lax.fori_loop(piece * k, piece * k + piece, pair_sum, 0)
+        for q in range(chunks * k, n_p if k == PIECES - 1 else chunks * k + chunks):
+
+            @pl.when(p != q)
+            def _():
+                to_plane(q, p).start()
+
+    for k in range(PIECES):
+        reduce_piece(k)
 
     for post in posts:
         post.wait_recv()
-    column = lax.rem(lane_16, 8)
+    column = lax.rem(lanes_of((8, 128)), 8)
     own = pack_out[...]
-    slab_l = jnp.where(column >= 4, own, pack_in[0])
-    slab_r = jnp.where(column < 4, own, pack_in[1])
-
-    def flat(slab, i):
-        return jnp.concatenate([slab[3 * i + t : 3 * i + t + 1] for t in range(3)], axis=1)
+    sides = (
+        (jnp.where(column >= 4, own, pack_in[0]), jnp.where(column >= 4, pack_in[4], pack_in[2])),
+        (jnp.where(column < 4, own, pack_in[1]), jnp.where(column < 4, pack_in[4], pack_in[3])),
+    )
+    lane_flat = lanes_of((1, 384))
+    blank = jnp.zeros((1, 128), f32)
+
+    def flat(side, i):
+        near, far = (part[2 * i : 2 * i + 2] for part in side)
+        inner = pltpu.roll(jnp.concatenate([near[0:1], near[1:2], blank], axis=1), 32, 1)
+        outer = jnp.concatenate([pltpu.roll(far[1:2], 32, 1), blank, pltpu.roll(far[0:1], 32, 1)], axis=1)
+        value = jnp.where((lane_flat >= 32) & (lane_flat < 288), inner, outer)
+        return jnp.where(lane_flat < 320, value, 0.0)
 
     def flat_both(i):
-        return jnp.concatenate([flat(slab_l, i), flat(slab_r, i)], axis=1)
+        return jnp.concatenate([flat(sides[0], i), flat(sides[1], i)], axis=1)
 
     field_s, cot_s, frozen_s = flat_both(0), flat_both(1), flat_both(2)
     masked_s = field_s * frozen_s
@@ -282,7 +306,8 @@
         xm[q] = jnp.zeros((96, 128), bf)
     one_rows([1, 2, 3, 36])
     one_rows([37, 38])
-    over_rows(one_rows)
+    over_rows(one_rows, 0, 4)
+    over_rows(one_rows, 4, 8)
 
     def second(windows, field, cot, frozen):
         two = jnp.tanh(dot(w2[...], windows)).astype(bf)
@@ -332,6 +357,34 @@
         to_along(lax.rem(z + offset, n_z), z).start()
     over_rows(two_rows, 4, 8)
 
+    def mid_rows(i, _):
+        rows = [4 + 8 * i + n for n in range(8)]
+        one = jnp.concatenate([xm[q, 32:64] for q in rows], axis=1)
+        acc_mid[...] += nt(windows_of(xd, rows), one)
+        return 0
+
+    lax.fori_loop(0, 4, mid_rows, 0)
+    for j in range(3):
+        b_rows[9 + 96 * (2 - j) : 9 + 96 * (2 - j) + 96, 0:32] = acc_mid[96 * j : 96 * j + 96]
+    rows = mine.shape[0]
+    layer = b_rows[pl.ds(0, rows, stride=4), :]
+    for g in range(1, 4):
+        layer = layer + pltpu.roll(b_rows[pl.ds(g, rows, stride=4), :], 32 * g, 1)
+    mine[...] = layer * scale
+    is_owner = (p < UNITS) & (lax.rem(p, 2) == core)
+
+    def to_owner(unit, slot):
+        return remote(mine.at[pl.ds(8 * unit, 8)], mine_x.at[slot], sem_l.at[unit], sem_lx.at[slot], plane(unit, unit % 2))
+
+    def is_other(unit):
+        return (p != unit) | (core != unit % 2)
+
+    for unit in range(UNITS):
+
+        @pl.when(is_other(unit))
+        def _():
+            to_owner(unit, n_p * core + p).start()
+
     def third(windows, one):
         one_f = one.astype(f32)
         d_one = dot(w3[...], windows) * (1.0 - one_f * one_f)
@@ -347,37 +400,30 @@
         for i, q in enumerate(rows):
             t_rows[pl.ds(pl.multiple_of(16 * q, 16), 16), :] = t_values[:, 128 * i : 128 * i + 128]
         if inner:
-            acc_mid[...] += nt(windows, one)
             values = jnp.concatenate([taps[pl.ds(pl.multiple_of(16 * q, 16), 16), :] for q in rows], axis=1)
             m_high, m_low = halves(values)
             parts = nt(jnp.concatenate([m_high, m_low], axis=0), jnp.concatenate([high, low], axis=0))
             parts = parts[0:16] + parts[16:32]
-            b_rows[0:9, 0:32] += (parts[:, 0:32] + parts[:, 32:64])[0:9]
-
+            b_in[0:9, 0:32] += (parts[:, 0:32] + parts[:, 32:64])[0:9]
+
+    b_in[...] = jnp.zeros(b_in.shape, f32)
     three_rows([3, 36], inner=False)
     over_rows(three_rows)
 
-    for j in range(3):
-        b_rows[9 + 96 * (2 - j) : 9 + 96 * (2 - j) + 96, 0:32] = acc_mid[96 * j : 96 * j + 96]
-    rows = mine.shape[0]
-    layer = b_rows[pl.ds(0, rows, stride=4), :]
+
+    late = b_in[pl.ds(0, 4, stride=4), :]
     for g in range(1, 4):
-        layer = layer + pltpu.roll(b_rows[pl.ds(g, rows, stride=4), :], 32 * g, 1)
-    mine[...] = layer * scale
-
-    is_owner = (p < UNITS) & (lax.rem(p, 2) == core)
-
-    def to_owner(unit, slot):
-        return remote(mine.at[pl.ds(8 * unit, 8)], mine_x.at[slot], sem_l.at[unit], sem_lx.at[slot], plane(unit, unit % 2))
-
-    def is_other(unit):
-        return (p != unit) | (core != unit % 2)
-
-    for unit in range(UNITS):
-
-        @pl.when(is_other(unit))
-        def _():
-            to_owner(unit, n_p * core + p).start()
+        late = late + pltpu.roll(b_in[pl.ds(g, 4, stride=4), :], 32 * g, 1)
+    me = n_p * core + p
+    late_x[me] = late * scale
+
+    def to_late(q, which, slot):
+        return remote(late_x.at[me], late_x.at[slot], sem_ls.at[which, q], sem_lr.at[slot], plane(q, which))
+
+    for offset in plane_order:
+        to_late(beside(*offset), core, me).start()
+        to_late(beside(*offset), other, me).start()
+    to_late(p, other, me).start()
 
     def column_sum(b):
         total = None
@@ -411,6 +457,20 @@
     fgrad_ref[0] = frozen * cot + unfrozen * cot * expo + frozen * d_masked
 
 
+    def to_along_mine(w, slot):
+        return remote(own_sum, mine_z.at[slot], sem_lz.at[0, w], sem_lz.at[1, slot], along(w))
+
+    @pl.when(is_owner)
+    def _():
+        def take(i, total):
+            slot = lax.rem(n_p * core + p + i, 2 * n_p)
+            to_owner(0, slot).wait_recv()
+            return total + mine_x[slot]
+
+        own_sum[...] = lax.fori_loop(1, 2 * n_p, take, mine[chunk(p, 8)])
+        for offset in line_order:
+            to_along_mine(lax.rem(z + offset, n_z), z).start()
+
     tile = lax.rem(z, 4)
 
     total = zs[tile].astype(f32)
@@ -421,27 +481,13 @@
     fin[core, chunk(4 * p + tile, 16)] = total.astype(bf)
 
     def to_four(i, slot):
-        w = z - tile + lax.rem(tile + i, 4)
+        w = lax.rem(z + n_z + (1, -1, -2)[i - 1], n_z)
         at = chunk(4 * p + slot, 16)
         return remote(fin.at[core, chunk(4 * p + tile, 16)], fin.at[core, at], sem_t.at[0, i], sem_t.at[1, slot], along(w))
 
     for i in range(1, 4):
         to_four(i, tile).start()
 
-    def to_along_mine(w, slot):
-        return remote(own_sum, mine_z.at[slot], sem_lz.at[0, w], sem_lz.at[1, slot], along(w))
-
-    @pl.when(is_owner)
-    def _():
-        def take(i, total):
-            slot = lax.rem(n_p * core + p + i, 2 * n_p)
-            to_owner(0, slot).wait_recv()
-            return total + mine_x[slot]
-
-        own_sum[...] = lax.fori_loop(1, 2 * n_p, take, mine[chunk(p, 8)])
-        for offset in line_order:
-            to_along_mine(lax.rem(z + offset, n_z), z).start()
-
     for i in range(1, 4):
         to_four(i, lax.rem(tile + i, 4)).wait_recv()
 
@@ -451,16 +497,25 @@
     def to_partner(which, slot):
         return remote(fin.at[core, chunk(slot)], fin.at[which, chunk(slot)], sem_b.at[0, slot], sem_b.at[1, slot], partner)
 
+    to_partner(core, p).start()
     for offset in plane_order:
         all_plane(beside(*offset), p).start()
-    to_partner(core, p).start()
-    for offset in plane_order:
-        q = from_beside(*offset)
-        all_plane(q, q).wait_recv()
-        to_partner(core, q).start()
+
+    def late_arrives(i, _):
+        to_late(p, other, lax.rem(me + i, 2 * n_p)).wait_recv()
+        return 0
+
+    lax.fori_loop(1, 2 * n_p, late_arrives, 0)
+    late_z[z] = lax.fori_loop(0, 2 * n_p, lambda i, total: total + late_x[i], jnp.zeros((4, 128), f32))
+
+    def late_along(w, slot):
+        return remote(late_z.at[z], late_z.at[slot], sem_lt.at[0, w], sem_lt.at[1, slot], along(w))
+
+    for offset in line_order:
+        late_along(lax.rem(z + offset, n_z), z).start()
 
     def to_all_mine(q, which, unit):
-        return remote(mine_fin.at[unit], mine_fin.at[unit], sem_la.at[which, q], sem_lr.at[unit], plane(q, which))
+        return remote(mine_fin.at[unit], mine_fin.at[unit], sem_la.at[which, q], sem_mr.at[unit], plane(q, which))
 
     @pl.when(is_owner)
     def _():
@@ -475,6 +530,18 @@
             to_all_mine(beside(*offset), other, p).start()
         to_all_mine(p, other, p).start()
 
+    for offset in plane_order:
+        q = from_beside(*offset)
+        all_plane(q, q).wait_recv()
+        to_partner(core, q).start()
+
+    def late_final(i, _):
+        w = lax.rem(z + i, n_z)
+        late_along(w, w).wait_recv()
+        return 0
+
+    lax.fori_loop(1, n_z, late_final, 0)
+    late_fin[...] = lax.fori_loop(0, n_z, lambda i, total: total + late_z[i], jnp.zeros((4, 128), f32))
     for q in range(n_p):
         to_partner(other, q).wait_recv()
     for unit in range(UNITS):
@@ -483,7 +550,7 @@
         def _():
             to_all_mine(p, other, unit).wait_recv()
 
-    for copy in (*swaps, *posts, halves_swap):
+    for copy in (*swaps, *posts, *pieces):
         copy.wait_send()
 
     def drain_plane(i, _):
@@ -496,13 +563,24 @@
         to_along(lax.rem(z + i, n_z), z).wait_send()
         return 0
 
-    def drain_partner(q, _):
-        to_partner(core, q).wait_send()
-        return 0
-
+    to_partner(core, p).wait_send()
+    for offset in plane_order:
+        to_partner(core, from_beside(*offset)).wait_send()
+    def drain_late(i, _):
+        q = lax.rem(p + i, n_p)
+        to_late(q, core, me).wait_send()
+        to_late(q, other, me).wait_send()
+        return 0
+
+    def drain_late_along(i, _):
+        late_along(lax.rem(z + i, n_z), z).wait_send()
+        return 0
+
+    lax.fori_loop(1, n_p, drain_late, 0)
+    to_late(p, other, me).wait_send()
+    lax.fori_loop(1, n_z, drain_late_along, 0)
     lax.fori_loop(1, n_p, drain_plane, 0)
     lax.fori_loop(1, n_z, drain_along, 0)
-    lax.fori_loop(0, n_p, drain_partner, 0)
     for i in range(1, 4):
         to_four(i, tile).wait_send()
     for unit in range(UNITS):
@@ -528,13 +606,14 @@
         to_all_mine(p, other, p).wait_send()
 
 
-def unpack_kernel(coupled_in, fgrad_in, fin, mine_fin, coupled_ref, fgrad_ref, out_ref, wide):
+def unpack_kernel(coupled_in, fgrad_in, fin, mine_fin, late_fin, coupled_ref, fgrad_ref, out_ref, wide):
     coupled_ref[...] = coupled_in[...]
     fgrad_ref[...] = fgrad_in[...]
     n_rows, n_cols = out_ref.shape
     share = n_rows // 2
     for unit in range(UNITS):
         wide[8 * unit : 8 * unit + 8] = mine_fin[unit]
+    wide[0:4] += late_fin[...]
     for which in range(2):
         base = 80 * (1 + (n_rows - 1 - share) * which)
 
@@ -554,7 +633,7 @@
     out_ref[:, 128 * whole :] = wide[pl.ds(whole, n_rows, stride=80), :][:, : n_cols - 128 * whole]
 
 
-def unpack_call(coupled, fgrad, fin, mine_fin, rows, cols):
+def unpack_call(coupled, fgrad, fin, mine_fin, late_fin, rows, cols):
     f32 = jnp.float32
     vmem = pl.BlockSpec(memory_space=pltpu.VMEM)
     return pl.pallas_call(
@@ -564,10 +643,10 @@
             jax.ShapeDtypeStruct(fgrad.shape, f32),
             jax.ShapeDtypeStruct((rows, cols), f32),
         ),
-        in_specs=[vmem] * 4,
+        in_specs=[vmem] * 5,
         out_specs=(vmem,) * 3,
         scratch_shapes=[pltpu.VMEM((80 * rows, 128), f32)],
-    )(coupled, fgrad, fin, mine_fin)
+    )(coupled, fgrad, fin, mine_fin, late_fin)
 
 
 def fused_call(scale, field, cot, checker, weight_in, weight_mid, weight_head, prior):
@@ -584,13 +663,14 @@
             jax.ShapeDtypeStruct(field.shape, f32),
             jax.ShapeDtypeStruct((2, n_p * 64, 128), bf),
             jax.ShapeDtypeStruct((UNITS, 8, 128), f32),
+            jax.ShapeDtypeStruct((4, 128), f32),
         ),
         in_specs=[vmem] * 6 + [pl.BlockSpec(memory_space=pl.ANY)],
-        out_specs=(vmem,) * 4,
+        out_specs=(vmem,) * 5,
         scratch_shapes=[
             pltpu.VMEM(field.shape, f32), pltpu.VMEM(field.shape, f32), pltpu.VMEM(checker.shape, jnp.int32),
             pltpu.VMEM((3, 48, 128), f32),
-            pltpu.VMEM((16, 128), f32), pltpu.VMEM((2, 16, 128), f32),
+            pltpu.VMEM((8, 128), f32), pltpu.VMEM((5, 8, 128), f32),
             pltpu.VMEM((640, 128), f32), pltpu.VMEM((16, 768), f32),
             pltpu.VMEM((16, 128), f32), pltpu.VMEM((32, 288), bf), pltpu.VMEM((32, 288), bf),
             pltpu.VMEM((40, 96, 128), bf), pltpu.VMEM((288, 768), bf),
@@ -604,8 +684,10 @@
             pltpu.VMEM((80, 128), f32),
             pltpu.VMEM((2 * n_p, 8, 128), f32), pltpu.VMEM((n_z, 8, 128), f32),
             pltpu.VMEM((8, 128), f32),
-            sem((2, 3)), sem((2, 2)), sem, sem((2,)), sem((2, n_p)), sem((2, n_z)), sem((2, 4)), sem((2, n_p)), sem((2, n_p)),
+            pltpu.VMEM((16, 128), f32), pltpu.VMEM((2 * n_p, 4, 128), f32), pltpu.VMEM((n_z, 4, 128), f32),
+            sem((2, 3)), sem((2, 5)), sem, sem((2, PIECES)), sem((2, n_p)), sem((2, n_z)), sem((2, 4)), sem((2, n_p)), sem((2, n_p)),
             sem((UNITS,)), sem((2 * n_p,)), sem((2, n_z)), sem((2, n_p)), sem((UNITS,)),
+            sem((2, n_p)), sem((2 * n_p,)), sem((2, n_z)),
         ],
         compiler_params=pltpu.CompilerParams(collective_id=0, has_side_effects=True),
     )(field, cot, checker, weight_in, weight_mid, weight_head, prior)

time: 56.5 us -> 53.6 us (0.949)
  Pallas kernels: 55.7 us -> 52.7 us
    pallas_call x1, Pallas kernels: 53 us -> 50.1 us  [fused_call(): pl.pallas_call(functools.partial(fused_kernel, scale), out_shape=(jax.Sha...]
where the time goes in v5:
time: 53.6 us; the launch traced here: 53.4 us
  Pallas kernels  52.7 us (98%)
  between operations  0.64 us (1%)
    pallas_call x1, Pallas kernels, fused_call(): pl.pallas_call(functools.partial(fused_kernel, scale), out_shape=(jax.Sha...  50.1 us
    pallas_call x1, Pallas kernels, unpack_call(): pl.pallas_call(unpack_kernel, out_shape=(jax.ShapeDtypeStruct(coupled.sha...  2.65 us

profile of v5, /device:TPU:1, one launch (start us, length us, event | category | flops | bytes accessed | tf_op | source)
XLA Modules:
  0.0 53.4 jit_solution(15606241934490419001)
XLA Ops:
  0.6 50.1 %shard_map.94 = (f32[1,32,128]{2,1,0:T(8,128)}, f32[1,32,128]{2,1,0:T(8,128)}, bf16[2,1024,128]{2,1,0:T(8,128)(2,1)}, f32[10,8,128]{2,1,0:T(8,128)}, f32[4,128]{1,0:T(4,128)}) custom-call(f32[1,32,128]{2,1,0:T(8,128)} %field_ref.1, f32[1,32,128]{2,1,0:T(8,128)} %cot_ref.1, s32[32,128]{1,0:T(8,128)} %check_ref.1, f32[3,3,32]{2,1,0:T(4,128)} %win_ref.1, ...), custom_call_target="tpu_custom_call" | custom-call | tf_op jit(solution)/shard_map/pallas_call | solution.py:659
  50.7 2.6 %shard_map.95 = (f32[1,32,128]{2,1,0:T(8,128)}, f32[1,32,128]{2,1,0:T(8,128)}, f32[24,9568]{1,0:T(8,128)}) custom-call(f32[1,32,128]{2,1,0:T(8,128)} %get-tuple-element.8.coupled_in, f32[1,32,128]{2,1,0:T(8,128)} %get-tuple-element.9.fgrad_in, bf16[2,1024,128]{2,1,0:T(8,128)(2,1)} %get-tuple-element.10.fin, f32[10,8,128]{2,1,0:T(8,128)} %get-tuple-element.11.mine_fin, ...), custom_call_target="tpu_custom_call" | custom-call | tf_op jit(solution)/shard_map/pallas_call | solution.py:639

commit v6 on v5

--- a/solution.py
+++ b/solution.py
@@ -295,9 +295,9 @@
         for i, q in enumerate(rows):
             spread_row(q, out[:, 128 * i : 128 * i + 128], False, xm)
 
-    def over_rows(step, first_group=0, last_group=8):
+    def over_rows(step, first_group=0, last_group=2):
         def body(i, _):
-            step([4 + 4 * i + n for n in range(4)])
+            step([4 + 16 * i + n for n in range(16)])
             return 0
 
         lax.fori_loop(first_group, last_group, body, 0)
@@ -306,8 +306,7 @@
         xm[q] = jnp.zeros((96, 128), bf)
     one_rows([1, 2, 3, 36])
     one_rows([37, 38])
-    over_rows(one_rows, 0, 4)
-    over_rows(one_rows, 4, 8)
+    over_rows(one_rows)
 
     def second(windows, field, cot, frozen):
         two = jnp.tanh(dot(w2[...], windows)).astype(bf)
@@ -345,7 +344,7 @@
     for q in (0, 1, 38, 39):
         xd[q] = jnp.zeros((96, 128), bf)
     two_rows([2, 3, 36, 37], inner=False)
-    over_rows(two_rows, 0, 4)
+    over_rows(two_rows, 0, 1)
     total = xs[chunk(p)].astype(f32)
     for offset in plane_order:
         q = from_beside(*offset)
@@ -355,15 +354,15 @@
 
     for offset in line_order:
         to_along(lax.rem(z + offset, n_z), z).start()
-    over_rows(two_rows, 4, 8)
+    over_rows(two_rows, 1, 2)
 
     def mid_rows(i, _):
-        rows = [4 + 8 * i + n for n in range(8)]
+        rows = [4 + 16 * i + n for n in range(16)]
         one = jnp.concatenate([xm[q, 32:64] for q in rows], axis=1)
         acc_mid[...] += nt(windows_of(xd, rows), one)
         return 0
 
-    lax.fori_loop(0, 4, mid_rows, 0)
+    lax.fori_loop(0, 2, mid_rows, 0)
     for j in range(3):
         b_rows[9 + 96 * (2 - j) : 9 + 96 * (2 - j) + 96, 0:32] = acc_mid[96 * j : 96 * j + 96]
     rows = mine.shape[0]

time: 53.6 us -> 51.2 us (0.955)
  Pallas kernels: 52.7 us -> 50.4 us
    pallas_call x1, Pallas kernels: 50.1 us -> 47.7 us  [fused_call(): pl.pallas_call(functools.partial(fused_kernel, scale), out_shape=(jax.Sha...]
where the time goes in v6:
time: 51.2 us; the launch traced here: 51 us
  Pallas kernels  50.4 us (98%)
  between operations  0.64 us (1%)
    pallas_call x1, Pallas kernels, fused_call(): pl.pallas_call(functools.partial(fused_kernel, scale), out_shape=(jax.Sha...  47.7 us
    pallas_call x1, Pallas kernels, unpack_call(): pl.pallas_call(unpack_kernel, out_shape=(jax.ShapeDtypeStruct(coupled.sha...  2.65 us

profile of v6, /device:TPU:1, one launch (start us, length us, event | category | flops | bytes accessed | tf_op | source)
XLA Modules:
  0.0 51.0 jit_solution(11284114561485432185)
XLA Ops:
  0.6 47.7 %shard_map.94 = (f32[1,32,128]{2,1,0:T(8,128)}, f32[1,32,128]{2,1,0:T(8,128)}, bf16[2,1024,128]{2,1,0:T(8,128)(2,1)}, f32[10,8,128]{2,1,0:T(8,128)}, f32[4,128]{1,0:T(4,128)}) custom-call(f32[1,32,128]{2,1,0:T(8,128)} %field_ref.1, f32[1,32,128]{2,1,0:T(8,128)} %cot_ref.1, s32[32,128]{1,0:T(8,128)} %check_ref.1, f32[3,3,32]{2,1,0:T(4,128)} %win_ref.1, ...), custom_call_target="tpu_custom_call" | custom-call | tf_op jit(solution)/shard_map/pallas_call | solution.py:658
  48.4 2.6 %shard_map.95 = (f32[1,32,128]{2,1,0:T(8,128)}, f32[1,32,128]{2,1,0:T(8,128)}, f32[24,9568]{1,0:T(8,128)}) custom-call(f32[1,32,128]{2,1,0:T(8,128)} %get-tuple-element.8.coupled_in, f32[1,32,128]{2,1,0:T(8,128)} %get-tuple-element.9.fgrad_in, bf16[2,1024,128]{2,1,0:T(8,128)(2,1)} %get-tuple-element.10.fin, f32[10,8,128]{2,1,0:T(8,128)} %get-tuple-element.11.mine_fin, ...), custom_call_target="tpu_custom_call" | custom-call | tf_op jit(solution)/shard_map/pallas_call | solution.py:638

commit v7 on v6

--- a/solution.py
+++ b/solution.py
@@ -621,14 +621,14 @@
             wide[pl.ds(pl.multiple_of(base + 80 * r, 16), 80)] = rows
             return 0
 
-        lax.fori_loop(0, share, widen, 0, unroll=2)
+        lax.fori_loop(0, share, widen, 0, unroll=4)
 
     def unpack(k, _):
         out_ref[:, pl.ds(pl.multiple_of(k * 128, 128), 128)] = wide[pl.ds(k, n_rows, stride=80), :]
         return 0
 
     whole = n_cols // 128
-    lax.fori_loop(0, whole, unpack, 0, unroll=2)
+    lax.fori_loop(0, whole, unpack, 0, unroll=37)
     out_ref[:, 128 * whole :] = wide[pl.ds(whole, n_rows, stride=80), :][:, : n_cols - 128 * whole]
 
 

time: 51.2 us -> 51 us (level)
  no operation moved by 1% of the time
where the time goes in v7:
time: 51 us; the launch traced here: 50.8 us
  Pallas kernels  50.2 us (98%)
  between operations  0.64 us (1%)
    pallas_call x1, Pallas kernels, fused_call(): pl.pallas_call(functools.partial(fused_kernel, scale), out_shape=(jax.Sha...  47.7 us
    pallas_call x1, Pallas kernels, unpack_call(): pl.pallas_call(unpack_kernel, out_shape=(jax.ShapeDtypeStruct(coupled.sha...  2.42 us

profile of v7, /device:TPU:1, one launch (start us, length us, event | category | flops | bytes accessed | tf_op | source)
XLA Modules:
  0.0 50.8 jit_solution(8805895140661556924)
XLA Ops:
  0.6 47.7 %shard_map.94 = (f32[1,32,128]{2,1,0:T(8,128)}, f32[1,32,128]{2,1,0:T(8,128)}, bf16[2,1024,128]{2,1,0:T(8,128)(2,1)}, f32[10,8,128]{2,1,0:T(8,128)}, f32[4,128]{1,0:T(4,128)}) custom-call(f32[1,32,128]{2,1,0:T(8,128)} %field_ref.1, f32[1,32,128]{2,1,0:T(8,128)} %cot_ref.1, s32[32,128]{1,0:T(8,128)} %check_ref.1, f32[3,3,32]{2,1,0:T(4,128)} %win_ref.1, ...), custom_call_target="tpu_custom_call" | custom-call | tf_op jit(solution)/shard_map/pallas_call | solution.py:658
  48.4 2.4 %shard_map.95 = (f32[1,32,128]{2,1,0:T(8,128)}, f32[1,32,128]{2,1,0:T(8,128)}, f32[24,9568]{1,0:T(8,128)}) custom-call(f32[1,32,128]{2,1,0:T(8,128)} %get-tuple-element.8.coupled_in, f32[1,32,128]{2,1,0:T(8,128)} %get-tuple-element.9.fgrad_in, bf16[2,1024,128]{2,1,0:T(8,128)(2,1)} %get-tuple-element.10.fin, f32[10,8,128]{2,1,0:T(8,128)} %get-tuple-element.11.mine_fin, ...), custom_call_target="tpu_custom_call" | custom-call | tf_op jit(solution)/shard_map/pallas_call | solution.py:638
